TPU v7x, 256 devices: a whole 4x4x8 slice. The times are simulated.
256 devices in a mesh: tok: 32 (over z, x), hid: 8 (over y, core).
Axes of the slice: x: 4, y: 4, z: 8, core: 2. Of those that a mesh axis runs over, the one named last changes fastest.
Arguments:
- inputs: float32 [4096, 4096], P('tok'), may hold values from -6 to 6
- cotangent: float32 [4096, 4096], P('tok'), may hold values from -6 to 6
- up_blocks: float32 [112, 4, 128, 128], P('hid', None, 'tok'), may hold values from -0.25 to 0.25
- down_blocks: float32 [112, 4, 128, 128], P('hid', None, 'tok'), may hold values from -0.25 to 0.25
- up_index: int32 [112, 4], P('hid'), may hold values from 0 to 31, all different within a row
- down_index: int32 [112, 4], P('hid'), may hold values from 0 to 31, all different within a row
- mom_up: float32 [112, 4, 128, 128], P('hid', None, 'tok'), may hold values from -6 to 6
- mom_down: float32 [112, 4, 128, 128], P('hid', None, 'tok'), may hold values from -6 to 6
Outputs:
- input_grad: float32 [4096, 4096], P('tok', 'hid')
- new_mom_up: float32 [112, 4, 128, 128], P('hid', None, 'tok')
- new_mom_down: float32 [112, 4, 128, 128], P('hid', None, 'tok')
Inputs may be any that keep to these rules, and one draw needn't show every extreme that they name: `up_index`: each row lists 4 different model blocks, and every model block appears in some row. `down_index`: each row lists 4 different model blocks, and every model block appears in some row.
All inputs are finite; a program needn't handle non-finite values.
Results may differ from a plain program's by a relative error of at most 0.0003.
Values sent between devices are 32-bit elements; how exact they have to be, the bound alone decides.
A program may use at most 64 MiB of HBM per device.

v0:
```python
import jax
import jax.numpy as jnp
from jax import lax
from jax.sharding import PartitionSpec as P


def shards(inputs, cotangent, up_blocks, down_blocks, up_index, down_index, mom_up, mom_down):
    highest = lax.Precision.HIGHEST
    row_count = inputs.shape[0]
    block = up_blocks.shape[3]
    block_count = inputs.shape[1] // block
    up_full, down_full = (
        lax.all_gather(up_blocks, "tok", axis=2, tiled=True),
        lax.all_gather(down_blocks, "tok", axis=2, tiled=True),
    )
    grad_scale = (row_count * lax.axis_size("tok")) ** (-0.5)
    x_blocks = inputs.reshape(row_count, block_count, block)
    cot_blocks = cotangent.reshape(row_count, block_count, block)
    x_sel = jnp.take(x_blocks, up_index, axis=1)
    cot_sel = jnp.take(cot_blocks, down_index, axis=1)
    pre_act = jnp.einsum("rfkd,fkdc->rfc", x_sel, up_full, precision=highest)
    sigmoid_pre = jax.nn.sigmoid(pre_act)
    activation = pre_act * sigmoid_pre
    grad_act = jnp.einsum("rfkd,fkcd->rfc", cot_sel, down_full, precision=highest)
    grad_pre = grad_act * sigmoid_pre * (1.0 + pre_act * (1.0 - sigmoid_pre))
    grad_down = grad_scale * jnp.einsum("rfc,rfkd->fkcd", activation, cot_sel, precision=highest)
    back_terms = jnp.einsum("rfc,fkdc->rfkd", grad_pre, up_full, precision=highest)
    onehot = (
        up_index[:, :, None] == jnp.arange(block_count, dtype=jnp.int32)[None, None, :]
    ).astype(jnp.float32)
    partial_value = jnp.einsum("rfkd,fkj->rjd", back_terms, onehot, precision=highest).reshape(
        row_count, -1
    )
    grad_up = grad_scale * jnp.einsum("rfkd,rfc->fkdc", x_sel, grad_pre, precision=highest)
    input_grad = lax.psum_scatter(partial_value, "hid", scatter_dimension=1, tiled=True)
    up_share, down_share = (
        lax.psum_scatter(grad_up, "tok", scatter_dimension=2, tiled=True),
        lax.psum_scatter(grad_down, "tok", scatter_dimension=2, tiled=True),
    )
    return (input_grad, 0.9 * mom_up + up_share, 0.9 * mom_down + down_share)


def solution(mesh):
    return jax.shard_map(
        shards,
        mesh=mesh,
        in_specs=(
            P("tok", None),
            P("tok", None),
            P("hid", None, "tok", None),
            P("hid", None, "tok", None),
            P("hid", None),
            P("hid", None),
            P("hid", None, "tok", None),
            P("hid", None, "tok", None),
        ),
        out_specs=(P("tok", "hid"), P("hid", None, "tok", None), P("hid", None, "tok", None)),
        check_vma=False,
    )
```

profile of v0, /device:TPU:32, one launch (start us, length us, event | category | flops | bytes accessed | tf_op | source)
XLA Modules:
  0.0 434.8 jit_solution(1202382156357738444)
XLA Ops:
  7.2 1.6 copy.59
  8.8 0.0 all-gather.3.cloned.1.call-start
  8.9 1.6 copy.51
  10.5 3.0 copy.47
  13.5 1.9 copy.49
  15.4 0.1 copy.48
  15.5 0.1 reshape.44
  15.6 2.7 gather_fusion
  18.3 5.3 %copy.50 = f32[14,4,128,128]{2,3,1,0:T(8,128)} copy(f32[14,4,128,128]{3,2,1,0:T(8,128)} %bitcast.75) | data formatting | bytes 7340032 | tf_op jit(solution)/shard_map/jit(_take)/gather | solution.py:20
  23.6 0.1 copy.46
  23.7 1.9 copy.55
  25.6 1.9 copy.57
  27.6 0.1 copy.56
  27.7 0.1 reshape.48
  27.8 2.7 gather_fusion.1
  30.5 5.1 %copy.58 = f32[14,4,128,128]{2,3,1,0:T(8,128)} copy(f32[14,4,128,128]{3,2,1,0:T(8,128)} %bitcast.76) | data formatting | bytes 7340032 | tf_op jit(solution)/shard_map/jit(_take)/gather | solution.py:19
  35.6 0.1 copy.54
  35.7 58.2 %all-gather.5.cloned.1.call-done = f32[14,4,128,128]{3,1,0,2:T(4,128)} async-done(((f32[14,4,4,128]{3,1,0,2:T(4,128)}), f32[14,4,128,128]{3,1,0,2:T(4,128)}) %all-gather.5.cloned.1.call-update) | async-done | bytes 3670032 | tf_op jit(solution)/shard_map/all_gather | solution.py:13
  93.9 9.6 %fusion.39 = f32[128,14,128]{2,0,1:T(8,128)S(1)} fusion(f32[14,4,128,128]{3,1,0,2:T(4,128)} %all-gather.5.cloned.1.call-done, f32[14,4,128,128]{2,3,1,0:T(8,128)} %copy.58, pred[14,4]{1,0:T(8,128)(4,1)S(1)} %copy.54), kind=kOutput, calls=%fused_computation.33 | convolution fusion | flops 1410203648 | bytes 8257592 | tf_op jit(solution)/shard_map/rfkd,fkdc->rfc/dot_general | solution.py:21
  103.6 5.5 %multiply_bitcast_fusion = f32[14,4,128,128]{2,3,1,0:T(8,128)} fusion(f32[14,4,128,128]{2,3,1,0:T(8,128)S(1)} %copy-done, pred[14,4]{1,0:T(8,128)(4,1)S(1)} %copy.46, f32[128,14,128]{2,0,1:T(8,128)S(1)} %fusion.39), kind=kOutput, calls=%fused_computation.13 | convolution fusion | flops 1412038656 | bytes 8257592 | tf_op jit(solution)/shard_map/rfc,rfkd->fkcd/dot_general | solution.py:26
  109.0 65.5 %all-gather.3.cloned.1.call-done = f32[14,4,128,128]{3,1,0,2:T(4,128)} async-done(((f32[14,4,4,128]{3,1,0,2:T(4,128)}), f32[14,4,128,128]{3,1,0,2:T(4,128)}) %all-gather.3.cloned.1.call-update) | async-done | bytes 3670032 | tf_op jit(solution)/shard_map/all_gather | solution.py:14
  174.5 9.8 %fusion.54 = f32[128,14,128,1]{2,0,3,1:T(8,128)S(1)} fusion(f32[14,4,128,128]{3,1,0,2:T(4,128)} %all-gather.3.cloned.1.call-done, f32[14,4,128,128]{2,3,1,0:T(8,128)} %copy.50, pred[14,4]{1,0:T(8,128)(4,1)S(1)} %copy.46, f32[128,14,128]{2,0,1:T(8,128)S(1)} %fusion.39), kind=kOutput, calls=%fused_computation.36 | convolution fusion | flops 1412038656 | bytes 9175096 | tf_op jit(solution)/shard_map/rfkd,fkcd->rfc/dot_general | solution.py:24
  184.3 5.3 %fusion.20 = f32[14,4,128,128]{3,2,1,0:T(8,128)} fusion(f32[128,14,128,1]{2,0,3,1:T(8,128)S(1)} %fusion.54, f32[14,4,128,128]{2,3,1,0:T(8,128)S(1)} %copy-done.1, pred[14,4]{1,0:T(8,128)(4,1)S(1)} %copy.54), kind=kOutput, calls=%fused_computation.22 | convolution fusion | flops 1411121152 | bytes 8257592 | tf_op jit(solution)/shard_map/rfkd,rfc->fkdc/dot_general | solution.py:34
  189.6 5.1 %copy.64 = f32[14,4,128,128]{3,2,1,0:T(8,128)} copy(f32[14,4,128,128]{2,3,1,0:T(8,128)} %multiply_bitcast_fusion) | data formatting | bytes 7340032 | tf_op jit(solution)/shard_map/mul | solution.py:26
  194.7 0.3 reduce-scatter.4.cloned.1.call-start
  195.0 6.0 %fusion.23 = f32[128,14,4,128]{3,0,2,1:T(8,128)S(1)} fusion(f32[128,14,128,1]{2,0,3,1:T(8,128)S(1)} %fusion.54, f32[14,4,128,128]{3,1,0,2:T(4,128)} %all-gather.5.cloned.1.call-done), kind=kOutput, calls=%fused_computation.23 | convolution fusion | flops 1409286144 | bytes 8257536 | tf_op jit(solution)/shard_map/rfc,fkdc->rfkd/dot_general | solution.py:27
  201.0 3.9 fusion
  204.9 3.0 copy.98
  208.0 0.6 dynamic-slice
  209.2 179.3 %all-reduce.5.cloned.1.call-done = (f32[14,4,128,128]{3,2,1,0:T(8,128)}, f32[14,4,128,128]{3,2,1,0:T(8,128)}) async-done(((f32[14,4,128,128]{3,2,1,0:T(8,128)}, f32[14,4,128,128]{3,2,1,0:T(8,128)}), (f32[14,4,128,128]{3,2,1,0:T(8,128)}, f32[14,4,128,128]{3,2,1,0:T(8,128)})) %all-reduce.5.cloned.1.call-update) | async-done | bytes 7340048
  388.5 1.8 dynamic-slice_add_fusion
  390.3 38.0 %reduce-scatter.4.cloned.1.call-done = f32[128,512]{1,0:T(8,128)} async-done(((f32[128,4096]{1,0:T(8,128)}), f32[128,512]{1,0:T(8,128)}) %reduce-scatter.4.cloned.1.call-update) | async-done | bytes 262160 | tf_op jit(solution)/shard_map/reduce_scatter | solution.py:35
  (28 shorter events, 0.2 us)
Async XLA Ops:
  7.2 86.7 %all-gather.5.cloned.1.call-start = ((), (), s32[]{:S(2)}) async-start(), calls=%async_computation.2 | async-start | bytes 3784704 | tf_op jit(solution)/shard_map/all_gather | solution.py:13
  8.8 165.7 %all-gather.3.cloned.1.call-start = ((), (), s32[]{:S(2)}) async-start(), calls=%async_computation.1 | async-start | bytes 3784704 | tf_op jit(solution)/shard_map/all_gather | solution.py:14
  10.5 5.0 %copy-start.6 = (s32[14,4]{0,1:T(4,128)S(1)}, s32[14,4]{0,1:T(4,128)}, u32[]{:S(2)}) copy-start(s32[14,4]{0,1:T(4,128)} %param.15) | copy-start | bytes 676
  10.5 378.0 %all-reduce.5.cloned.1.call-start = ((), (), s32[]{:S(2)}) async-start(), calls=%async_computation.4 | async-start | bytes 14680064
  18.3 5.4 %copy-start.2 = (f32[128,4096]{1,0:T(8,128)S(1)}, f32[128,4096]{1,0:T(8,128)}, u32[]{:S(2)}) copy-start(f32[128,4096]{1,0:T(8,128)} %param.10) | copy-start | bytes 6291460
  23.7 3.9 copy-start.5
  93.9 9.7 %copy-start = (f32[14,4,128,128]{2,3,1,0:T(8,128)S(1)}, f32[14,4,128,128]{2,3,1,0:T(8,128)}, u32[]{:S(2)}) copy-start(f32[14,4,128,128]{2,3,1,0:T(8,128)} %copy.50) | copy-start | bytes 11010052
  174.5 9.8 %copy-start.1 = (f32[14,4,128,128]{2,3,1,0:T(8,128)S(1)}, f32[14,4,128,128]{2,3,1,0:T(8,128)}, u32[]{:S(2)}) copy-start(f32[14,4,128,128]{2,3,1,0:T(8,128)} %copy.58) | copy-start | bytes 11010052
  194.7 233.5 %reduce-scatter.4.cloned.1.call-start = ((), (), s32[]{:S(2)}) async-start(), calls=%async_computation.3 | async-start | bytes 2359296 | tf_op jit(solution)/shard_map/reduce_scatter | solution.py:35
  204.9 3.1 copy-start.7
  204.9 183.6 %copy-start.3 = (f32[14,4,4,128]{3,2,1,0:T(4,128)S(1)}, f32[14,4,4,128]{3,2,1,0:T(4,128)}, u32[]{:S(2)}) copy-start(f32[14,4,4,128]{3,2,1,0:T(4,128)} %param.17) | copy-start | bytes 344068
  204.9 183.5 %copy-start.4 = (f32[14,4,4,128]{3,2,1,0:T(4,128)S(1)}, f32[14,4,4,128]{3,2,1,0:T(4,128)}, u32[]{:S(2)}) copy-start(f32[14,4,4,128]{3,2,1,0:T(4,128)} %param.16) | copy-start | bytes 344068
Sparse Core Ops, SparseCore 0:
  11.1 82.7 all-gather.4
  97.0 77.3 all-gather.2
  194.8 193.5 all-reduce.4
  391.4 36.7 reduce-scatter.3
where the time goes:
time: 436 us; the launch traced here: 435 us
  waiting for transfers between devices  341 us (78%)
  matrix products  40 us (9%)
  local copies, waits for them, and re-layouts  36.9 us (8%)
  between operations  14.6 us (3%)
    unnamed x5, waiting for transfers between devices  179 us
    all_gather x1, waiting for transfers between devices, shards(): lax.all_gather(down_blocks, 'tok', axis=2, tiled=True)  65.5 us
    all_gather x1, waiting for transfers between devices, shards(): lax.all_gather(up_blocks, 'tok', axis=2, tiled=True)  58.2 us
    reduce_scatter x1, waiting for transfers between devices, shards(): lax.psum_scatter(partial_value, 'hid', scatter_dimension=1, tiled=True)  38 us
    unnamed x22, local copies, waits for them, and re-layouts  11.6 us
    dot_general x1, matrix products, shards(): jnp.einsum('rfkd,fkcd->rfc', cot_sel, down_full, precision=highest)  9.77 us
    dot_general x1, matrix products, shards(): pre_act = jnp.einsum('rfkd,fkdc->rfc', x_sel, up_full, precision=highest)  9.65 us
  transfers between devices with their start and end apart: 4, of which 4 were waited for; matrix products, arithmetic and copies ran while one was open for 13% of the time, Pallas kernels for 0%

commit v1 on v0

v1 whole, which is shorter than its diff:
```python
import functools

import jax
import jax.numpy as jnp
from jax import lax
from jax.experimental import pallas as pl
from jax.experimental.pallas import tpu as pltpu
from jax.sharding import PartitionSpec as P

MESH = pl.DeviceIdType.MESH
NX, NY, NZ = 4, 4, 8
NF = 7
NA = 3
BF, F32 = jnp.bfloat16, jnp.float32


def split(a):
    hi = a.astype(BF)
    return hi, (a - hi.astype(F32)).astype(BF)


def dot3(a, b, dims):
    ah, al = a
    bh, bl = b
    d = functools.partial(lax.dot_general, dimension_numbers=(dims, ((), ())), preferred_element_type=F32)
    return d(ah, bh) + d(ah, bl) + d(al, bh)


def merge4(lo, a, b):
    ra, rb = pltpu.roll(a, 4, 1), pltpu.roll(b, 4, 1)
    return jnp.where(lo, a, rb), jnp.where(lo, ra, b)


def kernel(
    ui, di, slot, x_h, c_h, up_h, dn_h, mu_h, md_h,
    ig_out, mu_out, md_out,
    xo, xp, w, g, act, gpre, terms, ig,
    rau, rad, rbu, rbd, rx, rax, rc, cs, ryu, ryd, rp, mom,
    lsem, ssem, rsem,
):
    t, h = lax.axis_index("tok"), lax.axis_index("hid")
    z, x = t // NX, lax.rem(t, NX)
    y, c = h // 2, lax.rem(h, 2)
    hf = x // 2
    j = jnp.where((x == 1) | (x == 2), 1, 0)
    zz = lambda d: lax.rem(z + d + NZ, NZ)
    yy = lambda d: lax.rem(y + d + NY, NY)
    tok = lambda tz, tx: tz * NX + tx
    cross = (tok(z, 3 - x), h)
    inhalf = (tok(z, x + 1 - 2 * lax.rem(x, 2)), h)
    zup, zdn = (tok(zz(1), x), h), (tok(zz(-1), x), h)
    yup, ydn = (t, yy(1) * 2 + c), (t, yy(-1) * 2 + c)
    sib = (t, y * 2 + 1 - c)

    barrier = pltpu.get_barrier_semaphore()
    for dev in (cross, inhalf, zup, zdn, yup, ydn, sib):
        pl.semaphore_signal(barrier, inc=1, device_id=dev, device_id_type=MESH)

    nloc = [0]
    nrem = [0]
    pending = []

    def local(src, dst):
        cp = pltpu.make_async_copy(src, dst, lsem.at[nloc[0]])
        nloc[0] += 1
        cp.start()
        return cp

    def send(src, dst, dev, arrive=None):
        n = nrem[0]
        nrem[0] += 1
        cp = pltpu.make_async_remote_copy(src, dst, ssem.at[n], rsem.at[n], device_id=dev, device_id_type=MESH)
        cp.start()
        pending.append(cp)
        arrive = dst if arrive is None else arrive
        return pltpu.make_async_remote_copy(arrive, arrive, ssem.at[n], rsem.at[n], device_id=dev, device_id_type=MESH)

    lw = [
        local(up_h.at[pl.ds(NF * hf, NF)], w.at[z, j, hf, 0]),
        local(dn_h.at[pl.ds(NF * hf, NF)], w.at[z, j, hf, 1]),
    ]
    lx = [local(x_h, xo.at[0]), local(c_h, xo.at[1])]
    lm = [local(mu_h, mom.at[0]), local(md_h, mom.at[1])]

    pl.semaphore_wait(barrier, 7)

    oh = NF * (1 - hf)
    w0 = []
    for lo_f, n_f in ((0, NA), (NA, NF - NA)):
        for m, ref in enumerate((up_h, dn_h)):
            w0.append(
                send(
                    ref.at[pl.ds(oh + lo_f, n_f)],
                    w.at[z, j, hf, m, pl.ds(lo_f, n_f)],
                    cross,
                    w.at[z, j, 1 - hf, m, pl.ds(lo_f, n_f)],
                )
            )
    wa = lambda tz: w.at[tz, :, :, :, pl.ds(0, NA)]
    wah = lambda tz, jj: w.at[tz, jj, :, :, pl.ds(0, NA)]
    wb = lambda tz, jj: w.at[tz, jj, :, :, pl.ds(NA, NF - NA)]
    wbh = lambda tz, jj, m: w.at[tz, jj, m, :, pl.ds(NA, NF - NA)]

    tchunks = [(m, r) for m in range(2) for r in range(2)]
    RH = 8

    def share(m, r, ty, tc, sub=None):
        rows = pl.ds(r * RH, RH) if sub is None else pl.ds(r * RH + sub * (RH // 2), RH // 2)
        return xp.at[m, rows, pl.ds((tc * NY + ty) * 4, 4)]

    t0 = []
    for m, r in tchunks:
        src = (x_h, c_h)[m].at[pl.ds(r * RH, RH), pl.ds((c * NY + y) * 4, 4)]
        t0.append(send(src, share(m, r, y, c), cross))

    az, bz, bx, ty, tc = {}, {}, [], {}, []

    def a_ring(s):
        if s < NZ // 2 - 1:
            az[s] = (
                send(wa(zz(-s)), wa(zz(-s)), zup, wa(zz(-1 - s))),
                send(wa(zz(s)), wa(zz(s)), zdn, wa(zz(1 + s))),
            )
        else:
            az[s] = (
                send(wah(zz(-s), 0), wah(zz(-s), 0), zup, wah(zz(-1 - s), 0)),
                send(wah(zz(s), 1), wah(zz(s), 1), zdn, wah(zz(1 + s), 1)),
            )

    def b_ring(s):
        if s < NZ // 2 - 1:
            bz[s] = (
                send(wb(zz(-s), j), wb(zz(-s), j), zup, wb(zz(-1 - s), j)),
                send(wb(zz(s), j), wb(zz(s), j), zdn, wb(zz(1 + s), j)),
            )
        else:
            bz[s] = (
                send(wbh(zz(-s), j, 0), wbh(zz(-s), j, 0), zup, wbh(zz(-1 - s), j, 0)),
                send(wbh(zz(s), j, 1), wbh(zz(s), j, 1), zdn, wbh(zz(1 + s), j, 1)),
            )

    def b_x(d):
        bx.append(send(wb(zz(d), j), wb(zz(d), j), inhalf, wb(zz(d), 1 - j)))

    def t_core(k, d):
        m, r = tchunks[k]
        tc.append(send(share(m, r, yy(d), c), share(m, r, yy(d), c), sib, share(m, r, yy(d), 1 - c)))

    def t_ring(k, s):
        m, r = tchunks[k]
        if s == 0:
            ty[k, s] = (
                send(share(m, r, y, c), share(m, r, y, c), yup, share(m, r, yy(-1), c)),
                send(share(m, r, y, c), share(m, r, y, c), ydn, share(m, r, yy(1), c)),
            )
        else:
            ty[k, s] = (
                send(share(m, r, yy(-1), c, 0), share(m, r, yy(-1), c, 0), yup, share(m, r, yy(-2), c, 0)),
                send(share(m, r, yy(1), c, 1), share(m, r, yy(1), c, 1), ydn, share(m, r, yy(2), c, 1)),
            )

    def got(pair):
        for cp in pair:
            cp.wait_recv()

    def tok_own(k):
        t0[k].wait_recv()
        t_ring(k, 0)
        t_core(k, 0)

    def tok_mid(k):
        got(ty[k, 0])
        t_ring(k, 1)
        t_core(k, -1)
        t_core(k, 1)

    def tok_last(k):
        got(ty[k, 1])
        t_core(k, 2)

    def b_mid(s):
        got(bz[s])
        b_ring(s + 1)
        b_x(-1 - s)
        b_x(1 + s)

    def a_mid(s):
        got(az[s])
        a_ring(s + 1)

    for cp in lw:
        cp.wait()
    got(w0[:2])
    ax = send(wah(z, j), wah(z, j), inhalf, wah(z, 1 - j))
    got(w0[2:])
    b_ring(0)
    b_x(0)
    ax.wait_recv()
    a_ring(0)
    tok_own(0)
    b_mid(0)
    tok_own(1)
    a_mid(0)
    tok_own(2)
    tok_mid(0)
    b_mid(1)
    tok_own(3)
    a_mid(1)
    tok_mid(1)
    b_mid(2)
    tok_last(0)
    tok_mid(2)
    a_mid(2)
    tok_last(1)
    tok_mid(3)
    tok_last(2)
    got(bz[NZ // 2 - 1])
    b_x(NZ // 2)
    tok_last(3)
    got(az[NZ // 2 - 1])
    got(bx)
    got(tc)
    for cp in lx:
        cp.wait()

    lo = lax.broadcasted_iota(jnp.int32, (NZ, 8, 128), 1) < 4

    def weights(m, i):
        out = []
        for kp in range(2):
            x0, x3, x1, x2 = (w[:, jj, mm, m, i, kp] for jj in range(2) for mm in range(2))
            a0, b0 = merge4(lo, x0, x1)
            a1, b1 = merge4(lo, x2, x3)
            out += [jnp.stack([a0, a1], 1).reshape(128, 128), jnp.stack([b0, b1], 1).reshape(128, 128)]
        return out

    def tokens(m, idx, i):
        cols = []
        for k in range(4):
            b = idx[NF * hf + i, k]
            cols.append(jnp.concatenate([xo[m, :, b].reshape(128, 128), xp[m, :, b].reshape(128, 128)], 0))
        return split(jnp.concatenate(cols, 1))

    def forward(i, carry):
        wu = split(jnp.concatenate(weights(0, i), 0))
        wd = split(jnp.concatenate(weights(1, i), 1))
        pre = dot3(tokens(0, ui, i), wu, ((1,), (0,)))
        ga = dot3(tokens(1, di, i), wd, ((1,), (1,)))
        sg = 1.0 / (1.0 + jnp.exp(-pre))
        act[i] = pre * sg
        gp = ga * sg * (1.0 + pre * (1.0 - sg))
        gpre[i] = gp
        back = dot3(split(gp), wu, ((1,), (1,)))
        for k in range(4):
            terms[i * 4 + k] = back[:, k * 128 : (k + 1) * 128]
        return carry

    terms[4 * NF] = jnp.zeros((256, 128), F32)
    lax.fori_loop(0, NF, forward, 0)

    def gather_terms(b, carry):
        total = terms[slot[NF * hf, b]]
        for i in range(1, NF):
            total = total + terms[slot[NF * hf + i, b]]
        ig[b // 8, lax.rem(b // 4, 2), lax.rem(b, 4)] = total
        return carry

    lax.fori_loop(0, 32, gather_terms, 0)

    yorder = (2, 1, -1, 0)
    core = [send(ig.at[yy(d), 1 - c], cs.at[n], sib) for n, d in enumerate(yorder)]

    def grads(i, carry):
        gp = split(gpre[i])
        ac = split(act[i])
        gu = dot3(tokens(0, ui, i), gp, ((0,), (0,)))
        gd = dot3(ac, tokens(1, di, i), ((0,), (0,)))
        for m, full in enumerate((gu, gd)):
            for kp in range(2):
                if m == 0:
                    k0, k1 = (full[(2 * kp + e) * 128 : (2 * kp + e + 1) * 128] for e in range(2))
                else:
                    k0, k1 = (full[:, (2 * kp + e) * 128 : (2 * kp + e + 1) * 128] for e in range(2))
                k0, k1 = k0.reshape(NZ, 2, 8, 128), k1.reshape(NZ, 2, 8, 128)
                x0, x1 = merge4(lo, k0[:, 0], k1[:, 0])
                x2, x3 = merge4(lo, k0[:, 1], k1[:, 1])
                g[:, 0, 0, m, i, kp] = x0
                g[:, 1, 0, m, i, kp] = x1
                g[:, 1, 1, m, i, kp] = x2
                g[:, 0, 1, m, i, kp] = x3
        return carry

    lax.fori_loop(0, NF, grads, 0)

    A, B = pl.ds(0, NA), pl.ds(NA, NF - NA)
    zorder = [NZ // 2]
    for d in range(NZ // 2 - 1, 0, -1):
        zorder += [d, -d]
    zorder.append(0)
    xs = {d: send(g.at[zz(d), 1 - j, :, :, B], rx.at[n], inhalf) for n, d in enumerate(zorder)}
    ar, br, yr = {}, {}, {}

    def ra_ring(s):
        d = NZ // 2 - s
        if s == 0:
            ar[s] = (
                send(g.at[zz(d), 0, :, :, A], rau.at[0, 0], zup),
                send(g.at[zz(-d), 1, :, :, A], rad.at[0, 1], zdn),
            )
            return
        got(ar[s - 1])
        if s == 1:
            g[zz(d), 0, :, :, A] += rau[0, 0]
            g[zz(-d), 1, :, :, A] += rad[0, 1]
        else:
            g[zz(d), :, :, :, A] += rau[s - 1]
            g[zz(-d), :, :, :, A] += rad[s - 1]
        ar[s] = (
            send(g.at[zz(d), :, :, :, A], rau.at[s], zup),
            send(g.at[zz(-d), :, :, :, A], rad.at[s], zdn),
        )

    def add_x(d):
        xs[d].wait_recv()
        g[zz(d), j, :, :, B] += rx[zorder.index(d)]

    def rb_ring(s):
        d = NZ // 2 - s
        add_x(d)
        if s == 0:
            br[s] = (
                send(g.at[zz(d), j, 0, :, B], rbu.at[0, 0], zup),
                send(g.at[zz(-d), j, 1, :, B], rbd.at[0, 1], zdn),
            )
            return
        add_x(-d)
        got(br[s - 1])
        if s == 1:
            g[zz(d), j, 0, :, B] += rbu[0, 0]
            g[zz(-d), j, 1, :, B] += rbd[0, 1]
        else:
            g[zz(d), j, :, :, B] += rbu[s - 1]
            g[zz(-d), j, :, :, B] += rbd[s - 1]
        br[s] = (
            send(g.at[zz(d), j, :, :, B], rbu.at[s], zup),
            send(g.at[zz(-d), j, :, :, B], rbd.at[s], zdn),
        )

    def add_core(n):
        core[n].wait_recv()
        for b in range(4):
            ig[yy(yorder[n]), c, b] += cs[n, b]

    ra_ring(0)
    add_core(0)
    yr[0] = (
        send(ig.at[yy(2), c, pl.ds(0, 2)], ryu.at[0, pl.ds(0, 2)], yup),
        send(ig.at[yy(-2), c, pl.ds(2, 2)], ryd.at[0, pl.ds(2, 2)], ydn),
    )
    rb_ring(0)
    ra_ring(1)
    add_core(1)
    add_core(2)
    got(yr[0])
    for b in range(2):
        ig[yy(1), c, b] += ryu[0, b]
        ig[yy(-1), c, 2 + b] += ryd[0, 2 + b]
    yr[1] = (
        send(ig.at[yy(1), c], ryu.at[1], yup),
        send(ig.at[yy(-1), c], ryd.at[1], ydn),
    )
    rb_ring(1)
    ra_ring(2)
    add_core(3)
    rb_ring(2)
    ra_ring(3)
    got(yr[1])
    for b in range(4):
        ig[y, c, b] += ryu[1, b] + ryd[1, b]
    pair = send(ig.at[y, c, :, pl.ds(128, 128)], rp, cross)
    rb_ring(3)
    last = NZ // 2 - 1
    got(ar[last])
    g[z, :, :, :, A] += rau[last] + rad[last]
    axs = send(g.at[z, 1 - j, :, :, A], rax, inhalf)
    pair.wait_recv()
    for b in range(4):
        ig_out[:, b * 128 : (b + 1) * 128] = ig[y, c, b, 0:128] + rp[b]
    axs.wait_recv()
    g[z, j, :, :, A] += rax[...]
    ca = send(g.at[z, j, 1 - hf, :, A], rc.at[:, A], cross)
    add_x(0)
    got(br[last])
    g[z, j, :, :, B] += rbu[last] + rbd[last]
    cb = send(g.at[z, j, 1 - hf, :, B], rc.at[:, B], cross)
    for cp in lm:
        cp.wait()
    scale = 1.0 / 64.0
    for m, out in enumerate((mu_out, md_out)):
        out[pl.ds(NF * hf, NF)] = 0.9 * mom[m, pl.ds(NF * hf, NF)] + scale * g[z, j, hf, m]
    ca.wait_recv()
    cb.wait_recv()
    for m, out in enumerate((mu_out, md_out)):
        out[pl.ds(oh, NF)] = 0.9 * mom[m, pl.ds(oh, NF)] + scale * rc[m]
    for cp in pending:
        cp.wait_send()


def shards(inputs, cotangent, up_blocks, down_blocks, up_index, down_index, mom_up, mom_down):
    f, kb, r, b = up_blocks.shape
    tiles = lambda a: a.reshape(f, kb // 2, 2 * r, b)
    hit = up_index[:, :, None] == jnp.arange(32, dtype=jnp.int32)
    pos = 4 * (jnp.arange(f, dtype=jnp.int32) % NF)[:, None, None] + jnp.arange(kb, dtype=jnp.int32)[None, :, None]
    slot = jnp.min(jnp.where(hit, pos, 4 * NF), axis=1)
    rows8 = lambda a: a.reshape(16, 8, 32, b).transpose(0, 2, 1, 3)
    vm = lambda *s: pltpu.VMEM(s, F32)
    hbm, smem = pl.BlockSpec(memory_space=pl.ANY), pl.BlockSpec(memory_space=pltpu.SMEM)
    vmem = pl.BlockSpec(memory_space=pltpu.VMEM)
    tile = (2, 8, 128)
    ig, mu, md = pl.pallas_call(
        kernel,
        out_shape=(
            jax.ShapeDtypeStruct((128, 512), F32),
            jax.ShapeDtypeStruct((f, *tile), F32),
            jax.ShapeDtypeStruct((f, *tile), F32),
        ),
        in_specs=[smem] * 3 + [hbm] * 6,
        out_specs=(vmem, vmem, vmem),
        scratch_shapes=[
            vm(2, 16, 32, 8, 128),
            vm(2, 16, 32, 8, 128),
            vm(NZ, 2, 2, 2, NF, *tile),
            vm(NZ, 2, 2, 2, NF, *tile),
            vm(NF, 256, 128),
            vm(NF, 256, 128),
            vm(4 * NF + 1, 256, 128),
            vm(NY, 2, 4, 256, 128),
            vm(NZ // 2, 2, 2, 2, NA, *tile),
            vm(NZ // 2, 2, 2, 2, NA, *tile),
            vm(NZ // 2, 2, 2, NF - NA, *tile),
            vm(NZ // 2, 2, 2, NF - NA, *tile),
            vm(NZ, 2, 2, NF - NA, *tile),
            vm(2, 2, NA, *tile),
            vm(2, NF, *tile),
            vm(NY, 4, 256, 128),
            vm(2, 4, 256, 128),
            vm(2, 4, 256, 128),
            vm(4, 128, 128),
            vm(2, f, *tile),
            pltpu.SemaphoreType.DMA((6,)),
            pltpu.SemaphoreType.DMA((112,)),
            pltpu.SemaphoreType.DMA((112,)),
        ],
        compiler_params=pltpu.CompilerParams(
            collective_id=0, has_side_effects=True, vmem_limit_bytes=60 * 1024 * 1024
        ),
    )(up_index, down_index, slot, rows8(inputs), rows8(cotangent), tiles(up_blocks), tiles(down_blocks), tiles(mom_up), tiles(mom_down))
    return ig, mu.reshape(mom_up.shape), md.reshape(mom_down.shape)


def solution(mesh):
    return jax.shard_map(
        shards,
        mesh=mesh,
        in_specs=(
            P("tok", None),
            P("tok", None),
            P("hid", None, "tok", None),
            P("hid", None, "tok", None),
            P("hid", None),
            P("hid", None),
            P("hid", None, "tok", None),
            P("hid", None, "tok", None),
        ),
        out_specs=(P("tok", "hid"), P("hid", None, "tok", None), P("hid", None, "tok", None)),
        check_vma=False,
    )
```

time: 436 us -> 105 us (0.24)
  waiting for transfers between devices: 341 us -> 0 us
  Pallas kernels: 0 us -> 95.2 us
  matrix products: 40 us -> 0 us
  local copies, waits for them, and re-layouts: 36.9 us -> 6.91 us
  between operations: 14.6 us -> 0.65 us
    unnamed x5 -> x0, waiting for transfers between devices: 179 us -> none
    all_gather x2 -> x0, waiting for transfers between devices: 124 us -> none  [the longest x1 65.5 us: shards(): lax.all_gather(down_blocks, 'tok', axis=2, tiled=True)]
    pallas_call x0 -> x1, Pallas kernels: none -> 95.2 us  [shards(): pl.pallas_call(kernel, out_shape=(jax.ShapeDtypeStruct((128, 512), F32),...]
    dot_general x6 -> x0, matrix products: 40 us -> none  [the longest x1 9.77 us: shards(): jnp.einsum('rfkd,fkcd->rfc', cot_sel, down_full, precision=highest)]
    reduce_scatter x1 -> x0, waiting for transfers between devices: 38 us -> none  [shards(): lax.psum_scatter(partial_value, 'hid', scatter_dimension=1, tiled=True)]
    gather x4 -> x0, local copies, waits for them, and re-layouts: 15.8 us -> none  [the longest x2 7.94 us: shards(): cot_sel = jnp.take(cot_blocks, down_index, axis=1)]
    mul x1 -> x0, local copies, waits for them, and re-layouts: 5.11 us -> none  [shards(): grad_scale * jnp.einsum('rfc,rfkd->fkcd', activation, cot_sel, precision=...]
    unnamed x22 -> x7, local copies, waits for them, and re-layouts: 11.6 us -> 6.91 us
  transfers between devices with their start and end apart: 4 -> 0, of which waited for: 4 -> 0; matrix products, arithmetic and copies ran while one was open for 13% -> 0% of each run, Pallas kernels for 0% -> 0%
where the time goes in v1:
time: 105 us; the launch traced here: 104 us
  Pallas kernels  95.2 us (91%)
  local copies, waits for them, and re-layouts  6.91 us (7%)
    pallas_call x1, Pallas kernels, shards(): pl.pallas_call(kernel, out_shape=(jax.ShapeDtypeStruct((128, 512), F32),...  95.2 us
    unnamed x7, local copies, waits for them, and re-layouts  6.91 us

profile of v1, /device:TPU:32, one launch (start us, length us, event | category | flops | bytes accessed | tf_op | source)
XLA Modules:
  0.0 103.5 jit_solution(8016411999200389750)
XLA Ops:
  0.6 0.1 iota_add_fusion
  0.7 0.8 copy.15.ui
  1.5 0.0 copy-start
  1.5 0.7 select_reduce_fusion.slot
  2.2 1.4 %copy.16.di = s32[14,4]{1,0:T(8,128)} copy(s32[14,4]{0,1:T(4,128)} %param.13) | data formatting | bytes 448 | tf_op args[5]
  3.6 0.0 copy-done
  3.6 95.2 %shard_map.103 = (f32[128,512]{1,0:T(8,128)}, f32[14,2,8,128]{3,2,1,0:T(8,128)}, f32[14,2,8,128]{3,2,1,0:T(8,128)}) custom-call(s32[14,4]{1,0:T(8,128)} %copy-done, s32[14,4]{1,0:T(8,128)} %copy.16.di, s32[14,32]{1,0:T(8,128)} %select_reduce_fusion.slot, f32[16,32,8,128]{3,2,1,0:T(8,128)} %bitcast.12, f32[16,32,8,128]{3,2,1,0:T(8,128)} %bitcast.13, ...), custom_call_target="tpu_custom_call" | custom-call | tf_op jit(solution)/shard_map/pallas_call | solution.py:420
  98.7 1.7 %copy.20 = f32[128,512]{1,0:T(8,128)} copy(f32[128,512]{1,0:T(8,128)} %get-tuple-element.12) | data formatting | bytes 524288
  100.4 1.6 %copy.21 = f32[14,4,4,128]{3,2,1,0:T(4,128)} copy(f32[14,4,4,128]{3,2,1,0:T(4,128)} %bitcast.15) | data formatting | bytes 229376
  102.0 1.6 %copy.22 = f32[14,4,4,128]{3,2,1,0:T(4,128)} copy(f32[14,4,4,128]{3,2,1,0:T(4,128)} %bitcast.14) | data formatting | bytes 229376
  (1 shorter events, 0.0 us)
Async XLA Ops:
  1.5 2.1 %copy-start = (s32[14,4]{1,0:T(8,128)}, s32[14,4]{1,0:T(8,128)S(1)}, u32[]{:S(2)}) copy-start(s32[14,4]{1,0:T(8,128)S(1)} %copy.15.ui) | copy-start | bytes 676

commit v2 on v0

v2 whole, which is shorter than its diff:
```python
import functools
import heapq

import jax
import jax.numpy as jnp
from jax import lax
from jax.experimental import pallas as pl
from jax.experimental.pallas import tpu as pltpu
from jax.sharding import PartitionSpec as P

MESH = pl.DeviceIdType.MESH
NX, NY, NZ = 4, 4, 8
NF = 7
NA = 3
BF, F32 = jnp.bfloat16, jnp.float32


def split(a):
    hi = a.astype(BF)
    return hi, (a - hi.astype(F32)).astype(BF)


def dot3(a, b, dims):
    ah, al = a
    bh, bl = b
    d = functools.partial(lax.dot_general, dimension_numbers=(dims, ((), ())), preferred_element_type=F32)
    return d(ah, bh) + d(ah, bl) + d(al, bh)


def merge4(lo, a, b):
    ra, rb = pltpu.roll(a, 4, 1), pltpu.roll(b, 4, 1)
    return jnp.where(lo, a, rb), jnp.where(lo, ra, b)


class Plan:
    RATE = {"core": 250.0}
    LAT = {"core": 1.0, "cross": 1.9, "in": 1.9, "yu": 1.9, "yd": 1.9, "zu": 2.2, "zd": 2.2}

    def __init__(self, ssem, rsem, devs):
        self.ssem, self.rsem, self.devs = ssem, rsem, devs
        self.items, self.sent = [], []

    def send(self, name, link, src, dst, arrive, size, deps=(), land=None, before=None):
        self.items.append(dict(name=name, link=link, src=src, dst=dst, arrive=arrive, size=size, deps=set(deps), land=land, before=before))

    def step(self, name, cost, fn, deps=()):
        self.items.append(dict(name=name, link=None, cost=cost, fn=fn, deps=set(deps)))

    def issue(self, it):
        n = len(self.sent)
        if it["before"] is not None:
            it["before"]()
        mk = lambda s, d: pltpu.make_async_remote_copy(
            s, d, self.ssem.at[n], self.rsem.at[n], device_id=self.devs[it["link"]], device_id_type=MESH
        )
        cp = mk(it["src"], it["dst"])
        cp.start()
        self.sent.append(cp)
        return mk(it["arrive"], it["arrive"])

    def run(self):
        now, free, done, flying, todo, tick = 0.0, {}, set(), [], list(self.items), 0
        while todo or flying:
            for it in [i for i in todo if i["link"] and i["deps"] <= done]:
                todo.remove(it)
                handle = self.issue(it)
                end = max(now, free.get(it["link"], 0.0)) + it["size"] / 1e3 / self.RATE.get(it["link"], 46.0)
                free[it["link"]] = end
                heapq.heappush(flying, (end + self.LAT[it["link"]], tick, it, handle))
                tick += 1
            ready = next((i for i in todo if not i["link"] and i["deps"] <= done), None)
            if ready is not None and not (flying and flying[0][0] <= now):
                todo.remove(ready)
                ready["fn"]()
                now += ready["cost"]
                done.add(ready["name"])
                continue
            when, _, it, handle = heapq.heappop(flying)
            now = max(now, when)
            handle.wait_recv()
            if it["land"] is not None:
                it["land"]()
            done.add(it["name"])
        for cp in self.sent:
            cp.wait_send()


def kernel(
    ui, di, x_h, c_h, up_h, dn_h,
    ig_out, gu_out, gd_out,
    xo, xp, w, g, act, gpre, terms, ig,
    rau, rad, rbu, rbd, rx, rax, rc, cs, ryu, ryd, rp, slot,
    lsem, ssem, rsem,
):
    t, h = lax.axis_index("tok"), lax.axis_index("hid")
    z, x = t // NX, lax.rem(t, NX)
    y, c = h // 2, lax.rem(h, 2)
    hf = x // 2
    j = jnp.where((x == 1) | (x == 2), 1, 0)
    zz = lambda d: lax.rem(z + d + NZ, NZ)
    yy = lambda d: lax.rem(y + d + NY, NY)
    tok = lambda tz, tx: tz * NX + tx
    devs = {
        "cross": (tok(z, 3 - x), h),
        "in": (tok(z, x + 1 - 2 * lax.rem(x, 2)), h),
        "zu": (tok(zz(1), x), h),
        "zd": (tok(zz(-1), x), h),
        "yu": (t, yy(1) * 2 + c),
        "yd": (t, yy(-1) * 2 + c),
        "core": (t, y * 2 + 1 - c),
    }
    barrier = pltpu.get_barrier_semaphore()
    for dev in devs.values():
        pl.semaphore_signal(barrier, inc=1, device_id=dev, device_id_type=MESH)

    def local(n, src, dst):
        cp = pltpu.make_async_copy(src, dst, lsem.at[n])
        cp.start()
        return cp

    lw = [
        local(0, up_h.at[pl.ds(NF * hf, NF)], w.at[z, j, hf, 0]),
        local(1, dn_h.at[pl.ds(NF * hf, NF)], w.at[z, j, hf, 1]),
    ]
    lx = [local(2, x_h, xo.at[0]), local(3, c_h, xo.at[1])]
    for cp in lw:
        cp.wait()
    pl.semaphore_wait(barrier, len(devs))

    p = Plan(ssem, rsem, devs)
    A, B = pl.ds(0, NA), pl.ds(NA, NF - NA)
    KA, KB = NA * 16.384, (NF - NA) * 16.384
    KA, KB = KA * 1e3, KB * 1e3
    HZ = NZ // 2
    js, ms = (j, 1 - j), (hf, 1 - hf)
    oh = NF * (1 - hf)

    wA = lambda d, a, m: w.at[zz(d), js[a], ms[m], :, A]
    wB = lambda d, a, m: w.at[zz(d), js[a], ms[m], :, B]
    need_w = []

    def gather_ring(tag, ref, size, m, deps0):
        have = {0: deps0}
        for s in range(HZ):
            for link, sg in (("zu", -1), ("zd", 1)):
                if s == HZ - 1 and (m == 0) != (link == "zu"):
                    continue
                name = f"{tag}{m}{link}{s}"
                p.send(name, link, ref(sg * s), ref(sg * s), ref(sg * (s + 1)), size, have[sg * s])
                have[HZ if s == HZ - 1 else sg * (s + 1)] = [name]
                need_w.append(name)
        return have

    for m in range(2):
        p.send(f"ax{m}", "in", wA(0, 0, m), wA(0, 0, m), wA(0, 1, m), KA, [] if m == 0 else ["w0a0", "w0a1"])
        need_w.append(f"ax{m}")
        hb = gather_ring("b", lambda d, m=m: wB(d, 0, m), KB, m, [] if m == 0 else ["w0b0", "w0b1"])
        for d in (0, -1, 1, -2, 2, -3, 3, HZ):
            p.send(f"bx{m}{d}", "in", wB(d, 0, m), wB(d, 0, m), wB(d, 1, m), KB, hb[d])
            need_w.append(f"bx{m}{d}")
        gather_ring("a", lambda d, m=m: wA(d, 0, m), KA, m, [] if m == 0 else ["w0a0", "w0a1"])
        gather_ring("o", lambda d, m=m: wA(d, 1, m), KA, m, [f"ax{m}"])
        if m == 0:
            for tag, F, lo_f, n_f in (("b", B, NA, NF - NA), ("a", A, 0, NA)):
                for q, ref in enumerate((up_h, dn_h)):
                    p.send(
                        f"w0{tag}{q}", "cross", ref.at[pl.ds(oh + lo_f, n_f)],
                        w.at[z, j, hf, q, F], w.at[z, j, 1 - hf, q, F], n_f * 8192,
                    )

    RH = 4
    need_t = []
    KT = RH * 8 * 512 * 4

    def share(m, r, ty, tc, sub=None):
        rows = pl.ds(r * RH, RH) if sub is None else pl.ds(r * RH + sub * (RH // 2), RH // 2)
        return xp.at[m, rows, pl.ds((tc * NY + ty) * 4, 4)]

    for m in range(2):
        for r in range(16 // RH):
            k = f"{m}{r}"
            sh = lambda d, q=c, sub=None, m=m, r=r: share(m, r, yy(d), q, sub)
            src = (x_h, c_h)[m].at[pl.ds(r * RH, RH), pl.ds((c * NY + y) * 4, 4)]
            p.send(f"t{k}", "cross", src, sh(0), sh(0), KT)
            p.send(f"tyu{k}", "yu", sh(0), sh(0), sh(-1), KT, [f"t{k}"])
            p.send(f"tyd{k}", "yd", sh(0), sh(0), sh(1), KT, [f"t{k}"])
            p.send(f"tzu{k}", "yu", sh(-1, c, 0), sh(-1, c, 0), sh(-2, c, 0), KT // 2, [f"tyu{k}"])
            p.send(f"tzd{k}", "yd", sh(1, c, 1), sh(1, c, 1), sh(2, c, 1), KT // 2, [f"tyd{k}"])
            for d, dep in ((0, [f"t{k}"]), (-1, [f"tyu{k}"]), (1, [f"tyd{k}"]), (2, [f"tzu{k}", f"tzd{k}"])):
                p.send(f"tc{k}{d}", "core", sh(d), sh(d), sh(d, 1 - c), KT, dep)
                need_t.append(f"tc{k}{d}")

    def make_slots():
        for i in range(NF):
            picks = [ui[k, NF * hf + i] for k in range(4)]

            def one(b, carry, i=i, picks=picks):
                v = jnp.int32(4 * NF)
                for k in range(4):
                    v = jnp.where(picks[k] == b, 4 * i + k, v)
                slot[i, b] = v
                return carry

            lax.fori_loop(0, 32, one, 0)
        terms[4 * NF] = jnp.zeros((256, 128), F32)

    p.step("slots", 0.5, make_slots)
    lo = lax.broadcasted_iota(jnp.int32, (NZ, 8, 128), 1) < 4

    def weights(m, i):
        out = []
        for kp in range(2):
            x0, x3, x1, x2 = (w[:, jj, mm, m, i, kp] for jj in range(2) for mm in range(2))
            a0, b0 = merge4(lo, x0, x1)
            a1, b1 = merge4(lo, x2, x3)
            out += [jnp.stack([a0, a1], 1).reshape(128, 128), jnp.stack([b0, b1], 1).reshape(128, 128)]
        return out

    def tokens(m, idx, i):
        cols = []
        for k in range(4):
            b = idx[k, NF * hf + i]
            cols.append(jnp.concatenate([xo[m, :, b].reshape(128, 128), xp[m, :, b].reshape(128, 128)], 0))
        return split(jnp.concatenate(cols, 1))

    def forward(i, carry):
        wu = split(jnp.concatenate(weights(0, i), 0))
        wd = split(jnp.concatenate(weights(1, i), 1))
        pre = dot3(tokens(0, ui, i), wu, ((1,), (0,)))
        ga = dot3(tokens(1, di, i), wd, ((1,), (1,)))
        sg = 1.0 / (1.0 + jnp.exp(-pre))
        act[i] = pre * sg
        gp = ga * sg * (1.0 + pre * (1.0 - sg))
        gpre[i] = gp
        back = dot3(split(gp), wu, ((1,), (1,)))
        for k in range(4):
            terms[i * 4 + k] = back[:, k * 128 : (k + 1) * 128]
        return carry

    def gather_terms(b, carry):
        total = terms[slot[0, b]]
        for i in range(1, NF):
            total = total + terms[slot[i, b]]
        ig[b // 8, lax.rem(b // 4, 2), lax.rem(b, 4)] = total
        return carry

    def grads(i, carry):
        gp = split(gpre[i])
        ac = split(act[i])
        gu = dot3(tokens(0, ui, i), gp, ((0,), (0,)))
        gd = dot3(ac, tokens(1, di, i), ((0,), (0,)))
        for m, full in enumerate((gu, gd)):
            for kp in range(2):
                if m == 0:
                    k0, k1 = (full[(2 * kp + e) * 128 : (2 * kp + e + 1) * 128] for e in range(2))
                else:
                    k0, k1 = (full[:, (2 * kp + e) * 128 : (2 * kp + e + 1) * 128] for e in range(2))
                k0, k1 = k0.reshape(NZ, 2, 8, 128), k1.reshape(NZ, 2, 8, 128)
                x0, x1 = merge4(lo, k0[:, 0], k1[:, 0])
                x2, x3 = merge4(lo, k0[:, 1], k1[:, 1])
                g[:, 0, 0, m, i, kp] = x0
                g[:, 1, 0, m, i, kp] = x1
                g[:, 1, 1, m, i, kp] = x2
                g[:, 0, 1, m, i, kp] = x3
        return carry

    loop = lambda a, b, fn: lambda: lax.fori_loop(a, b, fn, 0) and None

    def wait_own():
        for cp in lx:
            cp.wait()

    p.step("own", 0.1, wait_own)
    p.step("fwd", 9.0, loop(0, NF, forward), need_w + need_t + ["own", "slots"])
    p.step("terms", 0.5, loop(0, 32, gather_terms), ["fwd"])

    KI = 2 * 256 * 128 * 4
    P2 = lambda b: pl.ds(2 * b, 2)

    def add_ig(d, b, buf):
        def fn():
            for e in range(2):
                ig[yy(d), c, 2 * b + e] += buf[e]

        return fn

    for n, d in enumerate((2, 1, -1, 0)):
        for b in range(2):
            p.send(
                f"c{d}{b}", "core", ig.at[yy(d), 1 - c, P2(b)], cs.at[n, P2(b)], cs.at[n, P2(b)], KI,
                ["terms"], add_ig(d, b, cs.at[n, P2(b)]),
            )
    for b in range(2):
        for link, sg, buf in (("yu", 1, ryu), ("yd", -1, ryd)):
            dep = [f"c{sg}{b}"]
            if (b == 0) == (link == "yu"):
                p.send(
                    f"y2{b}", link, ig.at[yy(2), c, P2(b)], buf.at[0, P2(b)], buf.at[0, P2(b)], KI, [f"c2{b}"],
                )
                dep.append(f"y2{b}")
                before = add_ig(sg, b, buf.at[0, P2(b)])
            else:
                before = None
            p.send(
                f"y1{link}{b}", link, ig.at[yy(sg), c, P2(b)], buf.at[1, P2(b)], buf.at[1, P2(b)], KI, dep,
                None, before,
            )

    def ig_sum(b):
        def fn():
            for e in range(2 * b, 2 * b + 2):
                ig[y, c, e] += ryu[1, e] + ryd[1, e]

        return fn

    def ig_final(b):
        def fn():
            for e in range(2 * b, 2 * b + 2):
                ig_out[:, e * 128 : (e + 1) * 128] = ig[y, c, e, 0:128] + rp[e]

        return fn

    for b in range(2):
        p.send(
            f"p{b}", "cross", ig.at[y, c, P2(b), pl.ds(128, 128)], rp.at[P2(b)], rp.at[P2(b)], KI // 2,
            [f"y1yu{b}", f"y1yd{b}", f"c0{b}"], ig_final(b), ig_sum(b),
        )

    p.step("gB", 2.1, loop(NA, NF, grads), ["terms"])
    p.step("gA", 1.6, loop(0, NA, grads), ["gB"])

    zorder = (HZ, 3, -3, 2, -2, 1, -1, 0)

    def add_to(ref, buf):
        def fn():
            ref[...] += buf[...]

        return fn

    gA = lambda d, a, m: g.at[zz(d), js[a], ms[m], :, A]
    gB = lambda d, a, m: g.at[zz(d), js[a], ms[m], :, B]
    for n, d in enumerate(zorder):
        for m in range(2):
            buf = rx.at[n, ms[m]]
            p.send(f"rx{m}{d}", "in", gB(d, 1, m), buf, buf, KB, ["gB"], add_to(gB(d, 0, m), buf))

    def reduce_ring(tag, ref, bufs, size, m, deps):
        for s in range(HZ):
            for link, sg in (("zu", 1), ("zd", -1)):
                if s == 0 and (m == 0) != (link == "zu"):
                    continue
                d = sg * (HZ - s)
                dep, before = list(deps(HZ if s == 0 else d)), None
                if s > 1 or (s == 1 and (m == 0) == (link == "zu")):
                    dep.append(f"{tag}{m}{link}{s - 1}")
                    before = add_to(ref(d), bufs[link](s - 1))
                p.send(f"{tag}{m}{link}{s}", link, ref(d), bufs[link](s), bufs[link](s), size, dep, None, before)
        return [f"{tag}{m}{link}{HZ - 1}" for link in ("zu", "zd")]

    def add2(ref, b1, b2):
        def fn():
            ref[...] += b1[...] + b2[...]

        return fn

    for m in range(2):
        bufs = {
            "zu": lambda s, m=m: rbu.at[s, ms[m]],
            "zd": lambda s, m=m: rbd.at[s, ms[m]],
        }
        fin = reduce_ring("B", lambda d, m=m: gB(d, 0, m), bufs, KB, m, lambda d, m=m: [f"rx{m}{d}"])
        p.step(f"finB{m}", 0.05, add2(gB(0, 0, m), bufs["zu"](HZ - 1), bufs["zd"](HZ - 1)), fin + [f"rx{m}0"])
    for m in range(2):
        for a in (1, 0):
            bufs = {
                "zu": lambda s, m=m, a=a: rau.at[s, js[a], ms[m]],
                "zd": lambda s, m=m, a=a: rad.at[s, js[a], ms[m]],
            }
            tag = "AO"[a]
            fin = reduce_ring(tag, lambda d, m=m, a=a: gA(d, a, m), bufs, KA, m, lambda d: ["gA"])
            p.step(f"fin{tag}{m}", 0.05, add2(gA(0, a, m), bufs["zu"](HZ - 1), bufs["zd"](HZ - 1)), fin)
        buf = rax.at[ms[m]]
        p.send(f"rax{m}", "in", gA(0, 1, m), buf, buf, KA, [f"finO{m}"])
        p.step(f"sumA{m}", 0.05, add_to(gA(0, 0, m), buf), [f"rax{m}", f"finA{m}"])
    p.send("cB", "cross", g.at[z, j, 1 - hf, :, B], rc.at[:, B], rc.at[:, B], KB, ["finB1"])
    p.send("cA", "cross", g.at[z, j, 1 - hf, :, A], rc.at[:, A], rc.at[:, A], KA, ["sumA1"])

    def own_out():
        for m, out in enumerate((gu_out, gd_out)):
            out[pl.ds(NF * hf, NF)] = g[z, j, hf, m]

    def other_out():
        for m, out in enumerate((gu_out, gd_out)):
            out[pl.ds(oh, NF)] = rc[m]

    p.step("own_out", 0.1, own_out, ["finB0", "sumA0"])
    p.step("other_out", 0.1, other_out, ["cA", "cB"])
    p.run()


def finish(ig, gu, gd, mu, md, ig_out, mu_out, md_out):
    ig_out[...] = ig[...]
    mu_out[...] = 0.9 * mu[...] + (1.0 / 64.0) * gu[...]
    md_out[...] = 0.9 * md[...] + (1.0 / 64.0) * gd[...]


def shards(inputs, cotangent, up_blocks, down_blocks, up_index, down_index, mom_up, mom_down):
    f, kb, r, b = up_blocks.shape
    tiles = lambda a: a.reshape(f, kb // 2, 2 * r, b)
    rows8 = lambda a: a.reshape(16, 8, 32, b).transpose(0, 2, 1, 3)
    vm = lambda *s: pltpu.VMEM(s, F32)
    hbm, smem = pl.BlockSpec(memory_space=pl.ANY), pl.BlockSpec(memory_space=pltpu.SMEM)
    vmem = pl.BlockSpec(memory_space=pltpu.VMEM)
    tile = (2, 8, 128)
    out_shape = (
        jax.ShapeDtypeStruct((128, 512), F32),
        jax.ShapeDtypeStruct((f, *tile), F32),
        jax.ShapeDtypeStruct((f, *tile), F32),
    )
    ig, gu, gd = pl.pallas_call(
        kernel,
        out_shape=out_shape,
        in_specs=[smem] * 2 + [hbm] * 4,
        out_specs=(vmem, vmem, vmem),
        scratch_shapes=[
            vm(2, 16, 32, 8, 128),
            vm(2, 16, 32, 8, 128),
            vm(NZ, 2, 2, 2, NF, *tile),
            vm(NZ, 2, 2, 2, NF, *tile),
            vm(NF, 256, 128),
            vm(NF, 256, 128),
            vm(4 * NF + 1, 256, 128),
            vm(NY, 2, 4, 256, 128),
            vm(NZ // 2, 2, 2, 2, NA, *tile),
            vm(NZ // 2, 2, 2, 2, NA, *tile),
            vm(NZ // 2, 2, 2, NF - NA, *tile),
            vm(NZ // 2, 2, 2, NF - NA, *tile),
            vm(NZ, 2, 2, NF - NA, *tile),
            vm(2, 2, NA, *tile),
            vm(2, NF, *tile),
            vm(NY, 4, 256, 128),
            vm(2, 4, 256, 128),
            vm(2, 4, 256, 128),
            vm(4, 128, 128),
            pltpu.SMEM((NF, 32), jnp.int32),
            pltpu.SemaphoreType.DMA((4,)),
            pltpu.SemaphoreType.DMA((256,)),
            pltpu.SemaphoreType.DMA((256,)),
        ],
        compiler_params=pltpu.CompilerParams(
            collective_id=0, has_side_effects=True, vmem_limit_bytes=60 * 1024 * 1024
        ),
    )(up_index.T, down_index.T, rows8(inputs), rows8(cotangent), tiles(up_blocks), tiles(down_blocks))
    ig, mu, md = pl.pallas_call(finish, out_shape=out_shape, in_specs=[vmem] * 5, out_specs=(vmem,) * 3)(
        ig, gu, gd, tiles(mom_up), tiles(mom_down)
    )
    return ig, mu.reshape(mom_up.shape), md.reshape(mom_down.shape)


def solution(mesh):
    return jax.shard_map(
        shards,
        mesh=mesh,
        in_specs=(
            P("tok", None),
            P("tok", None),
            P("hid", None, "tok", None),
            P("hid", None, "tok", None),
            P("hid", None),
            P("hid", None),
            P("hid", None, "tok", None),
            P("hid", None, "tok", None),
        ),
        out_specs=(P("tok", "hid"), P("hid", None, "tok", None), P("hid", None, "tok", None)),
        check_vma=False,
    )
```

time: 436 us -> 95.2 us (0.22)
  waiting for transfers between devices: 341 us -> 0 us
  Pallas kernels: 0 us -> 92.9 us
  matrix products: 40 us -> 0 us
  local copies, waits for them, and re-layouts: 36.9 us -> 0 us
  between operations: 14.6 us -> 0.64 us
    unnamed x5 -> x0, waiting for transfers between devices: 179 us -> none
    all_gather x2 -> x0, waiting for transfers between devices: 124 us -> none  [the longest x1 65.5 us: shards(): lax.all_gather(down_blocks, 'tok', axis=2, tiled=True)]
    pallas_call x0 -> x2, Pallas kernels: none -> 92.9 us  [the longest x1 91 us: shards(): pl.pallas_call(kernel, out_shape=out_shape, in_specs=[smem] * 2 + [hbm] *...]
    dot_general x6 -> x0, matrix products: 40 us -> none  [the longest x1 9.77 us: shards(): jnp.einsum('rfkd,fkcd->rfc', cot_sel, down_full, precision=highest)]
    reduce_scatter x1 -> x0, waiting for transfers between devices: 38 us -> none  [shards(): lax.psum_scatter(partial_value, 'hid', scatter_dimension=1, tiled=True)]
    gather x4 -> x0, local copies, waits for them, and re-layouts: 15.8 us -> none  [the longest x2 7.94 us: shards(): cot_sel = jnp.take(cot_blocks, down_index, axis=1)]
    unnamed x22 -> x0, local copies, waits for them, and re-layouts: 11.6 us -> none
    mul x1 -> x0, local copies, waits for them, and re-layouts: 5.11 us -> none  [shards(): grad_scale * jnp.einsum('rfc,rfkd->fkcd', activation, cot_sel, precision=...]
  transfers between devices with their start and end apart: 4 -> 0, of which waited for: 4 -> 0; matrix products, arithmetic and copies ran while one was open for 13% -> 0% of each run, Pallas kernels for 0% -> 0%
where the time goes in v2:
time: 95.2 us; the launch traced here: 93.6 us
  Pallas kernels  92.9 us (98%)
    pallas_call x1, Pallas kernels, shards(): pl.pallas_call(kernel, out_shape=out_shape, in_specs=[smem] * 2 + [hbm] *...  91 us
    pallas_call x1, Pallas kernels, shards(): pl.pallas_call(finish, out_shape=out_shape, in_specs=[vmem] * 5, out_spec...  1.94 us

profile of v2, /device:TPU:32, one launch (start us, length us, event | category | flops | bytes accessed | tf_op | source)
XLA Modules:
  0.0 93.6 jit_solution(14657868138814306870)
XLA Ops:
  0.6 91.0 %shard_map.103 = (f32[128,512]{1,0:T(8,128)}, f32[14,2,8,128]{3,2,1,0:T(8,128)}, f32[14,2,8,128]{3,2,1,0:T(8,128)}) custom-call(s32[4,14]{1,0:T(4,128)} %bitcast.20, s32[4,14]{1,0:T(4,128)} %bitcast.21, f32[16,32,8,128]{3,2,1,0:T(8,128)} %bitcast.14, f32[16,32,8,128]{3,2,1,0:T(8,128)} %bitcast.15, f32[14,2,8,128]{3,2,1,0:T(8,128)} %bitcast.16, ...), custom_call_target="tpu_custom_call" | custom-call | tf_op jit(solution)/shard_map/pallas_call | solution.py:420
  91.6 1.9 %shard_map.104 = (f32[128,512]{1,0:T(8,128)}, f32[14,2,8,128]{3,2,1,0:T(8,128)}, f32[14,2,8,128]{3,2,1,0:T(8,128)}) custom-call(f32[128,512]{1,0:T(8,128)} %get-tuple-element.9.ig, f32[14,2,8,128]{3,2,1,0:T(8,128)} %get-tuple-element.10.gu, f32[14,2,8,128]{3,2,1,0:T(8,128)} %get-tuple-element.11.gd, f32[14,2,8,128]{3,2,1,0:T(8,128)} %bitcast.18, ...), custom_call_target="tpu_custom_call" | custom-call | tf_op jit(solution)/shard_map/pallas_call | solution.py:454

commit v3 on v2

v3 whole, which is shorter than its diff:
```python
import functools
import heapq

import jax
import jax.numpy as jnp
from jax import lax
from jax.experimental import pallas as pl
from jax.experimental.pallas import tpu as pltpu
from jax.sharding import PartitionSpec as P

MESH = pl.DeviceIdType.MESH
NX, NY, NZ = 4, 4, 8
NF = 7
CHUNKS = (((0, 2), (2, 2)), ((4, 1), (5, 2)))
NSEND, NRECV = 47, 113
DEPTH = 3.0
BF, F32 = jnp.bfloat16, jnp.float32


def split(a):
    hi = a.astype(BF)
    return hi, (a - hi.astype(F32)).astype(BF)


def dot3(a, b, dims):
    ah, al = a
    bh, bl = b
    d = functools.partial(lax.dot_general, dimension_numbers=(dims, ((), ())), preferred_element_type=F32)
    return d(ah, bh) + d(ah, bl) + d(al, bh)


def merge4(lo, a, b):
    ra, rb = pltpu.roll(a, 4, 1), pltpu.roll(b, 4, 1)
    return jnp.where(lo, a, rb), jnp.where(lo, ra, b)


class Plan:
    RATE = {"core": 500.0}
    LAT = {"core": 1.0, "cross": 1.9, "in": 1.9, "yu": 1.9, "yd": 1.9, "zu": 2.2, "zd": 2.2}

    def __init__(self, ssem, rsem, devs):
        self.ssem, self.rsem, self.devs = ssem, rsem, devs
        self.items = []

    def send(self, name, link, src, dst, arrive, size, deps=(), land=None, before=None, rank=0):
        self.items.append(
            dict(name=name, link=link, src=src, dst=dst, arrive=arrive, size=size, deps=set(deps), land=land, before=before, rank=rank)
        )

    def step(self, name, cost, fn, deps=(), rank=0):
        self.items.append(dict(name=name, link=None, cost=cost, fn=fn, deps=set(deps), rank=rank))

    def order(self):
        now, free, done, flying, tick, ops = 0.0, {}, set(), [], 0, []
        todo = sorted(self.items, key=lambda i: i["rank"])
        while todo or flying:
            for it in [i for i in todo if i["link"] and i["deps"] <= done]:
                if free.get(it["link"], 0.0) - now > DEPTH:
                    continue
                todo.remove(it)
                end = max(now, free.get(it["link"], 0.0)) + it["size"] / 1e3 / self.RATE.get(it["link"], 46.0)
                free[it["link"]] = it["end"] = end
                it["start"] = now
                ops.append(("send", it))
                heapq.heappush(flying, (end + self.LAT[it["link"]], tick, it))
                tick += 1
            ready = next((i for i in todo if not i["link"] and i["deps"] <= done), None)
            if ready is not None and not (flying and flying[0][0] <= now):
                todo.remove(ready)
                ops.append(("step", ready))
                now += ready["cost"]
                done.add(ready["name"])
                continue
            when, _, it = heapq.heappop(flying)
            now = max(now, when)
            ops.append(("recv", it))
            done.add(it["name"])
        return ops

    def semaphores(self, ops):
        back = {"zu": "zd", "zd": "zu", "yu": "yd", "yd": "yu"}
        sent_at = {id(it): n for n, (what, it) in enumerate(ops) if what == "send"}
        got_at = {id(it): n for n, (what, it) in enumerate(ops) if what == "recv"}
        nsend, nrecv, sends, recvs = 0, 0, [], {}
        for n, (what, it) in enumerate(ops):
            if what != "send":
                continue
            it["after"] = None
            old = next((o for o in sends if o["end"] + 2.0 < it["start"]), None)
            if old is None:
                it["ssem"] = nsend
                nsend += 1
            else:
                it["ssem"], it["after"] = old["ssem"], old
                sends.remove(old)
            sends.append(it)
            link = it["link"]
            echo = [sent_at[id(o)] for w2, o in ops[:n] if w2 == "recv" and o["link"] == back.get(link, link)]
            last = max(echo, default=-1)
            pool = recvs.setdefault(link, [])
            old = next((o for o in pool if got_at[id(o)] < last), None)
            if old is None:
                it["rsem"] = nrecv
                nrecv += 1
            else:
                it["rsem"] = old["rsem"]
                pool.remove(old)
            pool.append(it)
        return sends, nsend, nrecv

    def run(self):
        ops = self.order()
        rest, nsend, nrecv = self.semaphores(ops)
        assert nsend <= NSEND and nrecv <= NRECV, (nsend, nrecv)
        for what, it in ops:
            if what == "step":
                it["fn"]()
            elif what == "recv":
                it["wait"].wait_recv()
                if it["land"] is not None:
                    it["land"]()
            else:
                if it["before"] is not None:
                    it["before"]()
                if it["after"] is not None:
                    it["after"]["copy"].wait_send()
                it["copy"], it["wait"] = (
                    pltpu.make_async_remote_copy(
                        s, d, self.ssem.at[it["ssem"]], self.rsem.at[it["rsem"]],
                        device_id=self.devs[it["link"]], device_id_type=MESH,
                    )
                    for s, d in ((it["src"], it["dst"]), (it["arrive"], it["arrive"]))
                )
                it["copy"].start()
        for it in rest:
            it["copy"].wait_send()


def kernel(
    ui, di, x_h, c_h, up_h, dn_h,
    ig_out, gu_out, gd_out,
    xo, xp, w, g, act, gpre, terms, ig,
    rau, rad, rbu, rbd, rx, rax, rc, cs, ryu, ryd, rp, slot,
    lsem, ssem, rsem,
):
    t, h = lax.axis_index("tok"), lax.axis_index("hid")
    z, x = t // NX, lax.rem(t, NX)
    y, c = h // 2, lax.rem(h, 2)
    hf = x // 2
    j = jnp.where((x == 1) | (x == 2), 1, 0)
    zz = lambda d: lax.rem(z + d + NZ, NZ)
    yy = lambda d: lax.rem(y + d + NY, NY)
    tok = lambda tz, tx: tz * NX + tx
    devs = {
        "cross": (tok(z, 3 - x), h),
        "in": (tok(z, x + 1 - 2 * lax.rem(x, 2)), h),
        "zu": (tok(zz(1), x), h),
        "zd": (tok(zz(-1), x), h),
        "yu": (t, yy(1) * 2 + c),
        "yd": (t, yy(-1) * 2 + c),
        "core": (t, y * 2 + 1 - c),
    }
    barrier = pltpu.get_barrier_semaphore()
    for dev in devs.values():
        pl.semaphore_signal(barrier, inc=1, device_id=dev, device_id_type=MESH)

    def local(n, src, dst):
        cp = pltpu.make_async_copy(src, dst, lsem.at[n])
        cp.start()
        return cp

    lw = [
        local(0, up_h.at[pl.ds(NF * hf, NF)], w.at[z, j, hf, 0]),
        local(1, dn_h.at[pl.ds(NF * hf, NF)], w.at[z, j, hf, 1]),
    ]
    lx = [local(2, x_h, xo.at[0]), local(3, c_h, xo.at[1])]
    for cp in lw:
        cp.wait()
    pl.semaphore_wait(barrier, len(devs))

    p = Plan(ssem, rsem, devs)
    HZ = NZ // 2
    js, ms = (j, 1 - j), (hf, 1 - hf)
    oh = NF * (1 - hf)
    KF = 2 * 8192

    def weight_gather(q, rank):
        (a0, an), (b0, bn) = CHUNKS[q]
        A, B = pl.ds(a0, an), pl.ds(b0, bn)
        wA = lambda d, a, m: w.at[zz(d), js[a], ms[m], :, A]
        wB = lambda d, a, m: w.at[zz(d), js[a], ms[m], :, B]
        need = []

        def ring(tag, ref, size, m, deps0):
            have = {0: deps0}
            for s in range(HZ):
                for link, sg in (("zu", -1), ("zd", 1)):
                    if s == HZ - 1 and (m == 0) != (link == "zu"):
                        continue
                    name = f"g{q}{tag}{m}{link}{s}"
                    p.send(name, link, ref(sg * s), ref(sg * s), ref(sg * (s + 1)), size, have[sg * s], rank=rank)
                    have[HZ if s == HZ - 1 else sg * (s + 1)] = [name]
                    need.append(name)
            return have

        for m in range(2):
            w0a, w0b = ([], []) if m == 0 else ([f"w{q}a0", f"w{q}a1"], [f"w{q}b0", f"w{q}b1"])
            p.send(f"ax{q}{m}", "in", wA(0, 0, m), wA(0, 0, m), wA(0, 1, m), an * KF, w0a, rank=rank)
            need.append(f"ax{q}{m}")
            hb = ring("b", lambda d, m=m: wB(d, 0, m), bn * KF, m, w0b)
            for d in (0, -1, 1, -2, 2, -3, 3, HZ):
                p.send(f"bx{q}{m}{d}", "in", wB(d, 0, m), wB(d, 0, m), wB(d, 1, m), bn * KF, hb[d], rank=rank)
                need.append(f"bx{q}{m}{d}")
            ring("a", lambda d, m=m: wA(d, 0, m), an * KF, m, w0a)
            ring("o", lambda d, m=m: wA(d, 1, m), an * KF, m, [f"ax{q}{m}"])
            if m == 0:
                for tag, F, lo_f, n_f in (("b", B, b0, bn), ("a", A, a0, an)):
                    for e, ref in enumerate((up_h, dn_h)):
                        p.send(
                            f"w{q}{tag}{e}", "cross", ref.at[pl.ds(oh + lo_f, n_f)],
                            w.at[z, j, hf, e, F], w.at[z, j, 1 - hf, e, F], n_f * 8192, rank=rank,
                        )
        return need

    need_w = [weight_gather(0, 0), weight_gather(1, 2)]

    RH = 4
    need_t = []
    KT = RH * 8 * 512 * 4

    def share(m, r, ty, tc, sub=None):
        rows = pl.ds(r * RH, RH) if sub is None else pl.ds(r * RH + sub * (RH // 2), RH // 2)
        return xp.at[m, rows, pl.ds((tc * NY + ty) * 4, 4)]

    for m in range(2):
        for r in range(16 // RH):
            k = f"{m}{r}"
            sh = lambda d, q=c, sub=None, m=m, r=r: share(m, r, yy(d), q, sub)
            src = (x_h, c_h)[m].at[pl.ds(r * RH, RH), pl.ds((c * NY + y) * 4, 4)]
            p.send(f"t{k}", "cross", src, sh(0), sh(0), KT, rank=1 if r + 4 * m < 4 else 3)
            p.send(f"tyu{k}", "yu", sh(0), sh(0), sh(-1), KT, [f"t{k}"])
            p.send(f"tyd{k}", "yd", sh(0), sh(0), sh(1), KT, [f"t{k}"])
            p.send(f"tzu{k}", "yu", sh(-1, c, 0), sh(-1, c, 0), sh(-2, c, 0), KT // 2, [f"tyu{k}"])
            p.send(f"tzd{k}", "yd", sh(1, c, 1), sh(1, c, 1), sh(2, c, 1), KT // 2, [f"tyd{k}"])
            for d, dep in ((0, [f"t{k}"]), (-1, [f"tyu{k}"]), (1, [f"tyd{k}"]), (2, [f"tzu{k}", f"tzd{k}"])):
                p.send(f"tc{k}{d}", "core", sh(d), sh(d), sh(d, 1 - c), KT, dep)
                need_t.append(f"tc{k}{d}")

    def make_slots():
        for i in range(NF):
            picks = [ui[k, NF * hf + i] for k in range(4)]

            def one(b, carry, i=i, picks=picks):
                v = jnp.int32(4 * NF)
                for k in range(4):
                    v = jnp.where(picks[k] == b, 4 * i + k, v)
                slot[i, b] = v
                return carry

            lax.fori_loop(0, 32, one, 0)
        terms[4 * NF] = jnp.zeros((256, 128), F32)

    p.step("slots", 0.5, make_slots)
    lo = lax.broadcasted_iota(jnp.int32, (NZ, 8, 128), 1) < 4

    def weights(m, i):
        out = []
        for kp in range(2):
            x0, x3, x1, x2 = (w[:, jj, mm, m, i, kp] for jj in range(2) for mm in range(2))
            a0, b0 = merge4(lo, x0, x1)
            a1, b1 = merge4(lo, x2, x3)
            out += [jnp.stack([a0, a1], 1).reshape(128, 128), jnp.stack([b0, b1], 1).reshape(128, 128)]
        return out

    def tokens(m, idx, i):
        cols = []
        for k in range(4):
            b = idx[k, NF * hf + i]
            cols.append(jnp.concatenate([xo[m, :, b].reshape(128, 128), xp[m, :, b].reshape(128, 128)], 0))
        return split(jnp.concatenate(cols, 1))

    def forward(i, carry):
        wu = split(jnp.concatenate(weights(0, i), 0))
        wd = split(jnp.concatenate(weights(1, i), 1))
        pre = dot3(tokens(0, ui, i), wu, ((1,), (0,)))
        ga = dot3(tokens(1, di, i), wd, ((1,), (1,)))
        sg = 1.0 / (1.0 + jnp.exp(-pre))
        act[i] = pre * sg
        gp = ga * sg * (1.0 + pre * (1.0 - sg))
        gpre[i] = gp
        back = dot3(split(gp), wu, ((1,), (1,)))
        for k in range(4):
            terms[i * 4 + k] = back[:, k * 128 : (k + 1) * 128]
        return carry

    def gather_terms(b, carry):
        total = terms[slot[0, b]]
        for i in range(1, NF):
            total = total + terms[slot[i, b]]
        ig[b // 8, lax.rem(b // 4, 2), lax.rem(b, 4)] = total
        return carry

    def grads(i, carry):
        gp = split(gpre[i])
        ac = split(act[i])
        gu = dot3(tokens(0, ui, i), gp, ((0,), (0,)))
        gd = dot3(ac, tokens(1, di, i), ((0,), (0,)))
        for m, full in enumerate((gu, gd)):
            for kp in range(2):
                if m == 0:
                    k0, k1 = (full[(2 * kp + e) * 128 : (2 * kp + e + 1) * 128] for e in range(2))
                else:
                    k0, k1 = (full[:, (2 * kp + e) * 128 : (2 * kp + e + 1) * 128] for e in range(2))
                k0, k1 = k0.reshape(NZ, 2, 8, 128), k1.reshape(NZ, 2, 8, 128)
                x0, x1 = merge4(lo, k0[:, 0], k1[:, 0])
                x2, x3 = merge4(lo, k0[:, 1], k1[:, 1])
                g[:, 0, 0, m, i, kp] = x0
                g[:, 1, 0, m, i, kp] = x1
                g[:, 1, 1, m, i, kp] = x2
                g[:, 0, 1, m, i, kp] = x3
        return carry

    loop = lambda a, b, fn: lambda: lax.fori_loop(a, b, fn, 0) and None

    def wait_own():
        for cp in lx:
            cp.wait()

    p.step("own", 0.1, wait_own)
    chunk_fs = [[f for f0, n in ch for f in range(f0, f0 + n)] for ch in CHUNKS]
    for q, fs in enumerate(chunk_fs):
        for i in fs:
            p.step(f"fwd{i}", 1.3, loop(i, i + 1, forward), need_w[q] + need_t + ["own", "slots"], rank=10 + 2 * q)
        p.step(f"grad{q}", 0.55 * len(fs), [loop(f0, f0 + n, grads) for f0, n in ((fs[0], len(fs)),)][0],
               [f"fwd{i}" for i in fs] + (["terms"] if q else []), rank=11 + 3 * q)
    p.step("terms", 0.5, loop(0, 32, gather_terms), [f"fwd{i}" for i in range(NF)], rank=13)

    KI = 256 * 128 * 4

    def add_ig(d, b, buf):
        def fn():
            ig[yy(d), c, b] += buf[...]

        return fn

    for n, d in enumerate((2, 1, -1, 0)):
        for b in range(4):
            buf = cs.at[n, b]
            p.send(f"c{d}{b}", "core", ig.at[yy(d), 1 - c, b], buf, buf, KI, ["terms"], add_ig(d, b, buf), rank=20 + b % 2)
    for b in range(4):
        for link, sg, buf in (("yu", 1, ryu), ("yd", -1, ryd)):
            dep, before = [f"c{sg}{b}"], None
            if (b < 2) == (link == "yu"):
                p.send(f"y2{b}", link, ig.at[yy(2), c, b], buf.at[0, b], buf.at[0, b], KI, [f"c2{b}"], rank=20 + b % 2)
                dep.append(f"y2{b}")
                before = add_ig(sg, b, buf.at[0, b])
            p.send(f"y1{link}{b}", link, ig.at[yy(sg), c, b], buf.at[1, b], buf.at[1, b], KI, dep, None, before, rank=20 + b % 2)

    def ig_sum(b):
        def fn():
            ig[y, c, b] += ryu[1, b] + ryd[1, b]

        return fn

    def ig_final(b):
        def fn():
            ig_out[:, b * 128 : (b + 1) * 128] = ig[y, c, b, 0:128] + rp[b]

        return fn

    for b in range(4):
        p.send(
            f"p{b}", "cross", ig.at[y, c, b, pl.ds(128, 128)], rp.at[b], rp.at[b], KI // 2,
            [f"y1yu{b}", f"y1yd{b}", f"c0{b}"], ig_final(b), ig_sum(b), rank=20,
        )

    zorder = (HZ, 3, -3, 2, -2, 1, -1, 0)

    def add_to(ref, buf):
        def fn():
            ref[...] += buf[...]

        return fn

    def add2(ref, b1, b2):
        def fn():
            ref[...] += b1[...] + b2[...]

        return fn

    def weight_reduce(q, rank):
        (a0, an), (b0, bn) = CHUNKS[q]
        A, B = pl.ds(a0, an), pl.ds(b0, bn)
        ready = [f"grad{q}"]
        gA = lambda d, a, m: g.at[zz(d), js[a], ms[m], :, A]
        gB = lambda d, a, m: g.at[zz(d), js[a], ms[m], :, B]
        for n, d in enumerate(zorder):
            for m in range(2):
                buf = rx.at[n, ms[m], :, B]
                p.send(f"rx{q}{m}{d}", "in", gB(d, 1, m), buf, buf, bn * KF, ready, add_to(gB(d, 0, m), buf), rank=rank)

        def ring(tag, ref, bufs, size, m, deps):
            for s in range(HZ):
                for link, sg in (("zu", 1), ("zd", -1)):
                    if s == 0 and (m == 0) != (link == "zu"):
                        continue
                    d = sg * (HZ - s)
                    dep, before = list(deps(HZ if s == 0 else d)), None
                    if s > 1 or (s == 1 and (m == 0) == (link == "zu")):
                        dep.append(f"r{q}{tag}{m}{link}{s - 1}")
                        before = add_to(ref(d), bufs[link](s - 1))
                    p.send(f"r{q}{tag}{m}{link}{s}", link, ref(d), bufs[link](s), bufs[link](s), size, dep, None, before, rank=rank)
            return [f"r{q}{tag}{m}{link}{HZ - 1}" for link in ("zu", "zd")]

        for m in range(2):
            bufs = {
                "zu": lambda s, m=m: rbu.at[s, ms[m], :, B],
                "zd": lambda s, m=m: rbd.at[s, ms[m], :, B],
            }
            fin = ring("B", lambda d, m=m: gB(d, 0, m), bufs, bn * KF, m, lambda d, m=m: [f"rx{q}{m}{d}"])
            p.step(f"finB{q}{m}", 0.05, add2(gB(0, 0, m), bufs["zu"](HZ - 1), bufs["zd"](HZ - 1)), fin + [f"rx{q}{m}0"])
        for m in range(2):
            for a in (1, 0):
                bufs = {
                    "zu": lambda s, m=m, a=a: rau.at[s, js[a], ms[m], :, A],
                    "zd": lambda s, m=m, a=a: rad.at[s, js[a], ms[m], :, A],
                }
                tag = "AO"[a]
                fin = ring(tag, lambda d, m=m, a=a: gA(d, a, m), bufs, an * KF, m, lambda d: ready)
                p.step(f"fin{tag}{q}{m}", 0.05, add2(gA(0, a, m), bufs["zu"](HZ - 1), bufs["zd"](HZ - 1)), fin)
            buf = rax.at[ms[m], :, A]
            p.send(f"rax{q}{m}", "in", gA(0, 1, m), buf, buf, an * KF, [f"finO{q}{m}"], rank=rank - 1)
            p.step(f"sumA{q}{m}", 0.05, add_to(gA(0, 0, m), buf), [f"rax{q}{m}", f"finA{q}{m}"])
        p.send(f"cB{q}", "cross", g.at[z, j, 1 - hf, :, B], rc.at[:, B], rc.at[:, B], bn * KF, [f"finB{q}1"], rank=rank)
        p.send(f"cA{q}", "cross", g.at[z, j, 1 - hf, :, A], rc.at[:, A], rc.at[:, A], an * KF, [f"sumA{q}1"], rank=rank)
        return [f"finB{q}0", f"sumA{q}0"], [f"cB{q}", f"cA{q}"]

    outs = [weight_reduce(0, 30), weight_reduce(1, 32)]

    def own_out():
        for m, out in enumerate((gu_out, gd_out)):
            out[pl.ds(NF * hf, NF)] = g[z, j, hf, m]

    def other_out():
        for m, out in enumerate((gu_out, gd_out)):
            out[pl.ds(oh, NF)] = rc[m]

    p.step("own_out", 0.1, own_out, outs[0][0] + outs[1][0])
    p.step("other_out", 0.1, other_out, outs[0][1] + outs[1][1])
    p.run()


def finish(ig, gu, gd, mu, md, ig_out, mu_out, md_out):
    ig_out[...] = ig[...]
    mu_out[...] = 0.9 * mu[...] + (1.0 / 64.0) * gu[...]
    md_out[...] = 0.9 * md[...] + (1.0 / 64.0) * gd[...]


def shards(inputs, cotangent, up_blocks, down_blocks, up_index, down_index, mom_up, mom_down):
    f, kb, r, b = up_blocks.shape
    tiles = lambda a: a.reshape(f, kb // 2, 2 * r, b)
    rows8 = lambda a: a.reshape(16, 8, 32, b).transpose(0, 2, 1, 3)
    vm = lambda *s: pltpu.VMEM(s, F32)
    hbm, smem = pl.BlockSpec(memory_space=pl.ANY), pl.BlockSpec(memory_space=pltpu.SMEM)
    vmem = pl.BlockSpec(memory_space=pltpu.VMEM)
    tile = (2, 8, 128)
    out_shape = (
        jax.ShapeDtypeStruct((128, 512), F32),
        jax.ShapeDtypeStruct((f, *tile), F32),
        jax.ShapeDtypeStruct((f, *tile), F32),
    )
    ig, gu, gd = pl.pallas_call(
        kernel,
        out_shape=out_shape,
        in_specs=[smem] * 2 + [hbm] * 4,
        out_specs=(vmem, vmem, vmem),
        scratch_shapes=[
            vm(2, 16, 32, 8, 128),
            vm(2, 16, 32, 8, 128),
            vm(NZ, 2, 2, 2, NF, *tile),
            vm(NZ, 2, 2, 2, NF, *tile),
            vm(NF, 256, 128),
            vm(NF, 256, 128),
            vm(4 * NF + 1, 256, 128),
            vm(NY, 2, 4, 256, 128),
            vm(NZ // 2, 2, 2, 2, NF, *tile),
            vm(NZ // 2, 2, 2, 2, NF, *tile),
            vm(NZ // 2, 2, 2, NF, *tile),
            vm(NZ // 2, 2, 2, NF, *tile),
            vm(NZ, 2, 2, NF, *tile),
            vm(2, 2, NF, *tile),
            vm(2, NF, *tile),
            vm(NY, 4, 256, 128),
            vm(2, 4, 256, 128),
            vm(2, 4, 256, 128),
            vm(4, 128, 128),
            pltpu.SMEM((NF, 32), jnp.int32),
            pltpu.SemaphoreType.DMA((4,)),
            pltpu.SemaphoreType.DMA((NSEND,)),
            pltpu.SemaphoreType.DMA((NRECV,)),
        ],
        compiler_params=pltpu.CompilerParams(
            collective_id=0, has_side_effects=True, vmem_limit_bytes=60 * 1024 * 1024
        ),
    )(up_index.T, down_index.T, rows8(inputs), rows8(cotangent), tiles(up_blocks), tiles(down_blocks))
    ig, mu, md = pl.pallas_call(finish, out_shape=out_shape, in_specs=[vmem] * 5, out_specs=(vmem,) * 3)(
        ig, gu, gd, tiles(mom_up), tiles(mom_down)
    )
    return ig, mu.reshape(mom_up.shape), md.reshape(mom_down.shape)


def solution(mesh):
    return jax.shard_map(
        shards,
        mesh=mesh,
        in_specs=(
            P("tok", None),
            P("tok", None),
            P("hid", None, "tok", None),
            P("hid", None, "tok", None),
            P("hid", None),
            P("hid", None),
            P("hid", None, "tok", None),
            P("hid", None, "tok", None),
        ),
        out_specs=(P("tok", "hid"), P("hid", None, "tok", None), P("hid", None, "tok", None)),
        check_vma=False,
    )
```

time: 95.2 us -> 86.7 us (0.911); the launches traced: 93.6 us -> 86.4 us
  Pallas kernels: 92.9 us -> 85.7 us
    pallas_call x1, Pallas kernels: 91 us -> 83.8 us  [shards(): pl.pallas_call(kernel, out_shape=out_shape, in_specs=[smem] * 2 + [hbm] *...]
where the time goes in v3:
time: 86.7 us; the launch traced here: 86.4 us
  Pallas kernels  85.7 us (99%)
    pallas_call x1, Pallas kernels, shards(): pl.pallas_call(kernel, out_shape=out_shape, in_specs=[smem] * 2 + [hbm] *...  83.8 us
    pallas_call x1, Pallas kernels, shards(): pl.pallas_call(finish, out_shape=out_shape, in_specs=[vmem] * 5, out_spec...  1.94 us

profile of v3, /device:TPU:32, one launch (start us, length us, event | category | flops | bytes accessed | tf_op | source)
XLA Modules:
  0.0 86.4 jit_solution(5907143331566932374)
XLA Ops:
  0.6 83.8 %shard_map.103 = (f32[128,512]{1,0:T(8,128)}, f32[14,2,8,128]{3,2,1,0:T(8,128)}, f32[14,2,8,128]{3,2,1,0:T(8,128)}) custom-call(s32[4,14]{1,0:T(4,128)} %bitcast.20, s32[4,14]{1,0:T(4,128)} %bitcast.21, f32[16,32,8,128]{3,2,1,0:T(8,128)} %bitcast.14, f32[16,32,8,128]{3,2,1,0:T(8,128)} %bitcast.15, f32[14,2,8,128]{3,2,1,0:T(8,128)} %bitcast.16, ...), custom_call_target="tpu_custom_call" | custom-call | tf_op jit(solution)/shard_map/pallas_call | solution.py:472
  84.4 1.9 %shard_map.104 = (f32[128,512]{1,0:T(8,128)}, f32[14,2,8,128]{3,2,1,0:T(8,128)}, f32[14,2,8,128]{3,2,1,0:T(8,128)}) custom-call(f32[128,512]{1,0:T(8,128)} %get-tuple-element.9.ig, f32[14,2,8,128]{3,2,1,0:T(8,128)} %get-tuple-element.10.gu, f32[14,2,8,128]{3,2,1,0:T(8,128)} %get-tuple-element.11.gd, f32[14,2,8,128]{3,2,1,0:T(8,128)} %bitcast.18, ...), custom_call_target="tpu_custom_call" | custom-call | tf_op jit(solution)/shard_map/pallas_call | solution.py:506

commit v4 on v3

--- a/solution.py
+++ b/solution.py
@@ -12,8 +12,8 @@
 NX, NY, NZ = 4, 4, 8
 NF = 7
 CHUNKS = (((0, 2), (2, 2)), ((4, 1), (5, 2)))
-NSEND, NRECV = 47, 113
-DEPTH = 3.0
+NSEND, NRECV = 38, 94
+DEPTH = 1.5
 BF, F32 = jnp.bfloat16, jnp.float32
 
 
@@ -22,11 +22,12 @@
     return hi, (a - hi.astype(F32)).astype(BF)
 
 
-def dot3(a, b, dims):
-    ah, al = a
-    bh, bl = b
-    d = functools.partial(lax.dot_general, dimension_numbers=(dims, ((), ())), preferred_element_type=F32)
-    return d(ah, bh) + d(ah, bl) + d(al, bh)
+def dot(a, b, dims):
+    return lax.dot_general(a, b, (dims, ((), ())), preferred_element_type=F32)
+
+
+def fold(a):
+    return a[:, :128] + a[:, 128:]
 
 
 def merge4(lo, a, b):
@@ -139,8 +140,8 @@
 def kernel(
     ui, di, x_h, c_h, up_h, dn_h,
     ig_out, gu_out, gd_out,
-    xo, xp, w, g, act, gpre, terms, ig,
-    rau, rad, rbu, rbd, rx, rax, rc, cs, ryu, ryd, rp, slot,
+    xo, xp0, xp1, w, g, act, gpre, terms, ig,
+    rau, rad, rbu, rbd, rx, rax, rc, cs, ryu, ryd, rp, wuh, wul, slot,
     lsem, ssem, rsem,
 ):
     t, h = lax.axis_index("tok"), lax.axis_index("hid")
@@ -191,7 +192,7 @@
         wB = lambda d, a, m: w.at[zz(d), js[a], ms[m], :, B]
         need = []
 
-        def ring(tag, ref, size, m, deps0):
+        def ring(tag, ref, size, m, deps0, rank):
             have = {0: deps0}
             for s in range(HZ):
                 for link, sg in (("zu", -1), ("zd", 1)):
@@ -205,32 +206,32 @@
 
         for m in range(2):
             w0a, w0b = ([], []) if m == 0 else ([f"w{q}a0", f"w{q}a1"], [f"w{q}b0", f"w{q}b1"])
-            p.send(f"ax{q}{m}", "in", wA(0, 0, m), wA(0, 0, m), wA(0, 1, m), an * KF, w0a, rank=rank)
+            p.send(f"ax{q}{m}", "in", wA(0, 0, m), wA(0, 0, m), wA(0, 1, m), an * KF, w0a, rank=rank - 0.5)
             need.append(f"ax{q}{m}")
-            hb = ring("b", lambda d, m=m: wB(d, 0, m), bn * KF, m, w0b)
+            hb = ring("b", lambda d, m=m: wB(d, 0, m), bn * KF, m, w0b, rank + 0.15 - 0.1 * m)
             for d in (0, -1, 1, -2, 2, -3, 3, HZ):
                 p.send(f"bx{q}{m}{d}", "in", wB(d, 0, m), wB(d, 0, m), wB(d, 1, m), bn * KF, hb[d], rank=rank)
                 need.append(f"bx{q}{m}{d}")
-            ring("a", lambda d, m=m: wA(d, 0, m), an * KF, m, w0a)
-            ring("o", lambda d, m=m: wA(d, 1, m), an * KF, m, [f"ax{q}{m}"])
+            ring("a", lambda d, m=m: wA(d, 0, m), an * KF, m, w0a, rank + 0.3 - 0.1 * m)
+            ring("o", lambda d, m=m: wA(d, 1, m), an * KF, m, [f"ax{q}{m}"], rank + 0.1 - 0.1 * m)
             if m == 0:
                 for tag, F, lo_f, n_f in (("b", B, b0, bn), ("a", A, a0, an)):
                     for e, ref in enumerate((up_h, dn_h)):
                         p.send(
                             f"w{q}{tag}{e}", "cross", ref.at[pl.ds(oh + lo_f, n_f)],
-                            w.at[z, j, hf, e, F], w.at[z, j, 1 - hf, e, F], n_f * 8192, rank=rank,
+                            w.at[z, j, hf, e, F], w.at[z, j, 1 - hf, e, F], n_f * 8192, rank=rank - 0.1 * (tag == "a"),
                         )
         return need
 
     need_w = [weight_gather(0, 0), weight_gather(1, 2)]
 
     RH = 4
-    need_t = []
+    need_t = [], []
     KT = RH * 8 * 512 * 4
 
     def share(m, r, ty, tc, sub=None):
         rows = pl.ds(r * RH, RH) if sub is None else pl.ds(r * RH + sub * (RH // 2), RH // 2)
-        return xp.at[m, rows, pl.ds((tc * NY + ty) * 4, 4)]
+        return (xp0, xp1)[m].at[rows, pl.ds((tc * NY + ty) * 4, 4)]
 
     for m in range(2):
         for r in range(16 // RH):
@@ -244,7 +245,7 @@
             p.send(f"tzd{k}", "yd", sh(1, c, 1), sh(1, c, 1), sh(2, c, 1), KT // 2, [f"tyd{k}"])
             for d, dep in ((0, [f"t{k}"]), (-1, [f"tyu{k}"]), (1, [f"tyd{k}"]), (2, [f"tzu{k}", f"tzd{k}"])):
                 p.send(f"tc{k}{d}", "core", sh(d), sh(d), sh(d, 1 - c), KT, dep)
-                need_t.append(f"tc{k}{d}")
+                need_t[m].append(f"tc{k}{d}")
 
     def make_slots():
         for i in range(NF):
@@ -276,22 +277,29 @@
         cols = []
         for k in range(4):
             b = idx[k, NF * hf + i]
-            cols.append(jnp.concatenate([xo[m, :, b].reshape(128, 128), xp[m, :, b].reshape(128, 128)], 0))
+            cols.append(jnp.concatenate([xo[m, :, b].reshape(128, 128), (xp0, xp1)[m][:, b].reshape(128, 128)], 0))
         return split(jnp.concatenate(cols, 1))
 
-    def forward(i, carry):
-        wu = split(jnp.concatenate(weights(0, i), 0))
-        wd = split(jnp.concatenate(weights(1, i), 1))
-        pre = dot3(tokens(0, ui, i), wu, ((1,), (0,)))
-        ga = dot3(tokens(1, di, i), wd, ((1,), (1,)))
+    def before(i):
+        wh, wl = split(jnp.concatenate(weights(0, i), 0))
+        wuh[i], wul[i] = wh, wl
+        xh, xl = tokens(0, ui, i)
+        act[i] = fold(dot(xh, jnp.concatenate([wh, wl], 1), ((1,), (0,)))) + dot(xl, wh, ((1,), (0,)))
+
+    def after(i):
+        wh, wl = split(jnp.concatenate(weights(1, i), 1))
+        ch, cl = tokens(1, di, i)
+        ga = fold(dot(ch, jnp.concatenate([wh, wl], 0), ((1,), (1,)))) + dot(cl, wh, ((1,), (1,)))
+        pre = act[i]
         sg = 1.0 / (1.0 + jnp.exp(-pre))
         act[i] = pre * sg
         gp = ga * sg * (1.0 + pre * (1.0 - sg))
         gpre[i] = gp
-        back = dot3(split(gp), wu, ((1,), (1,)))
+        gh, gl = split(gp)
+        uh, ul = wuh[i], wul[i]
+        back = dot(jnp.concatenate([gh, gl], 1), jnp.concatenate([uh, uh], 1), ((1,), (1,))) + dot(gh, ul, ((1,), (1,)))
         for k in range(4):
             terms[i * 4 + k] = back[:, k * 128 : (k + 1) * 128]
-        return carry
 
     def gather_terms(b, carry):
         total = terms[slot[0, b]]
@@ -301,10 +309,13 @@
         return carry
 
     def grads(i, carry):
-        gp = split(gpre[i])
-        ac = split(act[i])
-        gu = dot3(tokens(0, ui, i), gp, ((0,), (0,)))
-        gd = dot3(ac, tokens(1, di, i), ((0,), (0,)))
+        gh, gl = split(gpre[i])
+        ah, al = split(act[i])
+        xh, xl = tokens(0, ui, i)
+        ch, cl = tokens(1, di, i)
+        d00 = ((0,), (0,))
+        gu = fold(dot(xh, jnp.concatenate([gh, gl], 1), d00)) + dot(xl, gh, d00)
+        gd = dot(ah, ch, d00) + dot(ah, cl, d00) + dot(al, ch, d00)
         for m, full in enumerate((gu, gd)):
             for kp in range(2):
                 if m == 0:
@@ -330,8 +341,9 @@
     chunk_fs = [[f for f0, n in ch for f in range(f0, f0 + n)] for ch in CHUNKS]
     for q, fs in enumerate(chunk_fs):
         for i in fs:
-            p.step(f"fwd{i}", 1.3, loop(i, i + 1, forward), need_w[q] + need_t + ["own", "slots"], rank=10 + 2 * q)
-        p.step(f"grad{q}", 0.55 * len(fs), [loop(f0, f0 + n, grads) for f0, n in ((fs[0], len(fs)),)][0],
+            p.step(f"pre{i}", 0.45, functools.partial(before, i), need_w[q] + need_t[0] + ["own", "slots"], rank=10 + 2 * q)
+            p.step(f"fwd{i}", 0.75, functools.partial(after, i), [f"pre{i}"] + need_t[1], rank=10 + 2 * q)
+        p.step(f"grad{q}", 0.5 * len(fs), [loop(f0, f0 + n, grads) for f0, n in ((fs[0], len(fs)),)][0],
                [f"fwd{i}" for i in fs] + (["terms"] if q else []), rank=11 + 3 * q)
     p.step("terms", 0.5, loop(0, 32, gather_terms), [f"fwd{i}" for i in range(NF)], rank=13)
 
@@ -399,7 +411,7 @@
                 buf = rx.at[n, ms[m], :, B]
                 p.send(f"rx{q}{m}{d}", "in", gB(d, 1, m), buf, buf, bn * KF, ready, add_to(gB(d, 0, m), buf), rank=rank)
 
-        def ring(tag, ref, bufs, size, m, deps):
+        def ring(tag, ref, bufs, size, m, deps, rank):
             for s in range(HZ):
                 for link, sg in (("zu", 1), ("zd", -1)):
                     if s == 0 and (m == 0) != (link == "zu"):
@@ -417,7 +429,7 @@
                 "zu": lambda s, m=m: rbu.at[s, ms[m], :, B],
                 "zd": lambda s, m=m: rbd.at[s, ms[m], :, B],
             }
-            fin = ring("B", lambda d, m=m: gB(d, 0, m), bufs, bn * KF, m, lambda d, m=m: [f"rx{q}{m}{d}"])
+            fin = ring("B", lambda d, m=m: gB(d, 0, m), bufs, bn * KF, m, lambda d, m=m: [f"rx{q}{m}{d}"], rank)
             p.step(f"finB{q}{m}", 0.05, add2(gB(0, 0, m), bufs["zu"](HZ - 1), bufs["zd"](HZ - 1)), fin + [f"rx{q}{m}0"])
         for m in range(2):
             for a in (1, 0):
@@ -426,7 +438,7 @@
                     "zd": lambda s, m=m, a=a: rad.at[s, js[a], ms[m], :, A],
                 }
                 tag = "AO"[a]
-                fin = ring(tag, lambda d, m=m, a=a: gA(d, a, m), bufs, an * KF, m, lambda d: ready)
+                fin = ring(tag, lambda d, m=m, a=a: gA(d, a, m), bufs, an * KF, m, lambda d: ready, rank + 5)
                 p.step(f"fin{tag}{q}{m}", 0.05, add2(gA(0, a, m), bufs["zu"](HZ - 1), bufs["zd"](HZ - 1)), fin)
             buf = rax.at[ms[m], :, A]
             p.send(f"rax{q}{m}", "in", gA(0, 1, m), buf, buf, an * KF, [f"finO{q}{m}"], rank=rank - 1)
@@ -476,7 +488,8 @@
         out_specs=(vmem, vmem, vmem),
         scratch_shapes=[
             vm(2, 16, 32, 8, 128),
-            vm(2, 16, 32, 8, 128),
+            vm(16, 32, 8, 128),
+            vm(16, 32, 8, 128),
             vm(NZ, 2, 2, 2, NF, *tile),
             vm(NZ, 2, 2, 2, NF, *tile),
             vm(NF, 256, 128),
@@ -494,6 +507,8 @@
             vm(2, 4, 256, 128),
             vm(2, 4, 256, 128),
             vm(4, 128, 128),
+            pltpu.VMEM((NF, 512, 128), BF),
+            pltpu.VMEM((NF, 512, 128), BF),
             pltpu.SMEM((NF, 32), jnp.int32),
             pltpu.SemaphoreType.DMA((4,)),
             pltpu.SemaphoreType.DMA((NSEND,)),

time: 86.7 us -> 83.4 us (0.962)
  Pallas kernels: 85.7 us -> 82.5 us
    pallas_call x1, Pallas kernels: 83.8 us -> 80.6 us  [shards(): pl.pallas_call(kernel, out_shape=out_shape, in_specs=[smem] * 2 + [hbm] *...]
where the time goes in v4:
time: 83.4 us; the launch traced here: 83.2 us
  Pallas kernels  82.5 us (99%)
    pallas_call x1, Pallas kernels, shards(): pl.pallas_call(kernel, out_shape=out_shape, in_specs=[smem] * 2 + [hbm] *...  80.6 us
    pallas_call x1, Pallas kernels, shards(): pl.pallas_call(finish, out_shape=out_shape, in_specs=[vmem] * 5, out_spec...  1.94 us

profile of v4, /device:TPU:32, one launch (start us, length us, event | category | flops | bytes accessed | tf_op | source)
XLA Modules:
  0.0 83.2 jit_solution(11983495996539053625)
XLA Ops:
  0.6 80.6 %shard_map.103 = (f32[128,512]{1,0:T(8,128)}, f32[14,2,8,128]{3,2,1,0:T(8,128)}, f32[14,2,8,128]{3,2,1,0:T(8,128)}) custom-call(s32[4,14]{1,0:T(4,128)} %bitcast.20, s32[4,14]{1,0:T(4,128)} %bitcast.21, f32[16,32,8,128]{3,2,1,0:T(8,128)} %bitcast.14, f32[16,32,8,128]{3,2,1,0:T(8,128)} %bitcast.15, f32[14,2,8,128]{3,2,1,0:T(8,128)} %bitcast.16, ...), custom_call_target="tpu_custom_call" | custom-call | tf_op jit(solution)/shard_map/pallas_call | solution.py:484
  81.2 1.9 %shard_map.104 = (f32[128,512]{1,0:T(8,128)}, f32[14,2,8,128]{3,2,1,0:T(8,128)}, f32[14,2,8,128]{3,2,1,0:T(8,128)}) custom-call(f32[128,512]{1,0:T(8,128)} %get-tuple-element.9.ig, f32[14,2,8,128]{3,2,1,0:T(8,128)} %get-tuple-element.10.gu, f32[14,2,8,128]{3,2,1,0:T(8,128)} %get-tuple-element.11.gd, f32[14,2,8,128]{3,2,1,0:T(8,128)} %bitcast.18, ...), custom_call_target="tpu_custom_call" | custom-call | tf_op jit(solution)/shard_map/pallas_call | solution.py:521

commit v5 on v4

--- a/solution.py
+++ b/solution.py
@@ -138,10 +138,10 @@
 
 
 def kernel(
-    ui, di, x_h, c_h, up_h, dn_h,
+    ui_h, di_h, x_h, c_h, up_h, dn_h,
     ig_out, gu_out, gd_out,
     xo, xp0, xp1, w, g, act, gpre, terms, ig,
-    rau, rad, rbu, rbd, rx, rax, rc, cs, ryu, ryd, rp, wuh, wul, slot,
+    rau, rad, rbu, rbd, rx, rax, rc, cs, ryu, ryd, rp, wuh, wul, slot, ui, di,
     lsem, ssem, rsem,
 ):
     t, h = lax.axis_index("tok"), lax.axis_index("hid")
@@ -170,6 +170,7 @@
         cp.start()
         return cp
 
+    li = [local(4, ui_h, ui), local(5, di_h, di)]
     lw = [
         local(0, up_h.at[pl.ds(NF * hf, NF)], w.at[z, j, hf, 0]),
         local(1, dn_h.at[pl.ds(NF * hf, NF)], w.at[z, j, hf, 1]),
@@ -248,6 +249,8 @@
                 need_t[m].append(f"tc{k}{d}")
 
     def make_slots():
+        for cp in li:
+            cp.wait()
         for i in range(NF):
             picks = [ui[k, NF * hf + i] for k in range(4)]
 
@@ -473,7 +476,7 @@
     tiles = lambda a: a.reshape(f, kb // 2, 2 * r, b)
     rows8 = lambda a: a.reshape(16, 8, 32, b).transpose(0, 2, 1, 3)
     vm = lambda *s: pltpu.VMEM(s, F32)
-    hbm, smem = pl.BlockSpec(memory_space=pl.ANY), pl.BlockSpec(memory_space=pltpu.SMEM)
+    hbm = pl.BlockSpec(memory_space=pl.ANY)
     vmem = pl.BlockSpec(memory_space=pltpu.VMEM)
     tile = (2, 8, 128)
     out_shape = (
@@ -483,8 +486,8 @@
     )
     ig, gu, gd = pl.pallas_call(
         kernel,
-        out_shape=out_shape,
-        in_specs=[smem] * 2 + [hbm] * 4,
+        out_shape=tuple(vm(*o.shape) for o in out_shape),
+        in_specs=[hbm] * 6,
         out_specs=(vmem, vmem, vmem),
         scratch_shapes=[
             vm(2, 16, 32, 8, 128),
@@ -510,7 +513,9 @@
             pltpu.VMEM((NF, 512, 128), BF),
             pltpu.VMEM((NF, 512, 128), BF),
             pltpu.SMEM((NF, 32), jnp.int32),
-            pltpu.SemaphoreType.DMA((4,)),
+            pltpu.SMEM((kb, f), jnp.int32),
+            pltpu.SMEM((kb, f), jnp.int32),
+            pltpu.SemaphoreType.DMA((6,)),
             pltpu.SemaphoreType.DMA((NSEND,)),
             pltpu.SemaphoreType.DMA((NRECV,)),
         ],
@@ -519,7 +524,7 @@
         ),
     )(up_index.T, down_index.T, rows8(inputs), rows8(cotangent), tiles(up_blocks), tiles(down_blocks))
     ig, mu, md = pl.pallas_call(finish, out_shape=out_shape, in_specs=[vmem] * 5, out_specs=(vmem,) * 3)(
-        ig, gu, gd, tiles(mom_up), tiles(mom_down)
+        *(pltpu.with_memory_space_constraint(a, pltpu.VMEM) for a in (ig, gu, gd)), tiles(mom_up), tiles(mom_down)
     )
     return ig, mu.reshape(mom_up.shape), md.reshape(mom_down.shape)
 

time: 83.4 us -> 81.7 us (0.980)
  Pallas kernels: 82.5 us -> 80.9 us
    pallas_call x1, Pallas kernels: 80.6 us -> 79.1 us  [shards(): pl.pallas_call(kernel, out_shape=tuple((vm(*o.shape) for o in out_shape))...]
where the time goes in v5:
time: 81.7 us; the launch traced here: 81.5 us
  Pallas kernels  80.9 us (99%)
    pallas_call x1, Pallas kernels, shards(): pl.pallas_call(kernel, out_shape=tuple((vm(*o.shape) for o in out_shape))...  79.1 us
    pallas_call x1, Pallas kernels, shards(): pl.pallas_call(finish, out_shape=out_shape, in_specs=[vmem] * 5, out_spec...  1.76 us

profile of v5, /device:TPU:32, one launch (start us, length us, event | category | flops | bytes accessed | tf_op | source)
XLA Modules:
  0.0 81.5 jit_solution(3939064547173277911)
XLA Ops:
  0.6 79.1 %shard_map.103 = (f32[128,512]{1,0:T(8,128)S(1)}, f32[14,2,8,128]{3,2,1,0:T(8,128)S(1)}, f32[14,2,8,128]{3,2,1,0:T(8,128)S(1)}) custom-call(s32[4,14]{1,0:T(4,128)} %bitcast.20, s32[4,14]{1,0:T(4,128)} %bitcast.21, f32[16,32,8,128]{3,2,1,0:T(8,128)} %bitcast.14, f32[16,32,8,128]{3,2,1,0:T(8,128)} %bitcast.15, f32[14,2,8,128]{3,2,1,0:T(8,128)} %bitcast.16, ...), custom_call_target="tpu_custom_call" | custom-call | tf_op jit(solution)/shard_map/pallas_call | solution.py:487
  79.8 1.8 %shard_map.104 = (f32[128,512]{1,0:T(8,128)}, f32[14,2,8,128]{3,2,1,0:T(8,128)}, f32[14,2,8,128]{3,2,1,0:T(8,128)}) custom-call(f32[128,512]{1,0:T(8,128)S(1)} %get-tuple-element.9.ig, f32[14,2,8,128]{3,2,1,0:T(8,128)S(1)} %get-tuple-element.10.gu, f32[14,2,8,128]{3,2,1,0:T(8,128)S(1)} %get-tuple-element.11.gd, f32[14,2,8,128]{3,2,1,0:T(8,128)} %bitcast.18, ...), custom_call_target="tpu_custom_call" | custom-call | tf_op jit(solution)/shard_map/pallas_call | solution.py:526

commit v6 on v5

--- a/solution.py
+++ b/solution.py
@@ -138,10 +138,10 @@
 
 
 def kernel(
-    ui_h, di_h, x_h, c_h, up_h, dn_h,
+    ui_h, di_h, x_h, c_h, up_h, dn_h, mu_h, md_h,
     ig_out, gu_out, gd_out,
     xo, xp0, xp1, w, g, act, gpre, terms, ig,
-    rau, rad, rbu, rbd, rx, rax, rc, cs, ryu, ryd, rp, wuh, wul, slot, ui, di,
+    rau, rad, rbu, rbd, rx, rax, rc, cs, ryu, ryd, rp, wuh, wul, slot, ui, di, mom,
     lsem, ssem, rsem,
 ):
     t, h = lax.axis_index("tok"), lax.axis_index("hid")
@@ -170,6 +170,7 @@
         cp.start()
         return cp
 
+    lm = [local(6, mu_h, mom.at[0]), local(7, md_h, mom.at[1])]
     li = [local(4, ui_h, ui), local(5, di_h, di)]
     lw = [
         local(0, up_h.at[pl.ds(NF * hf, NF)], w.at[z, j, hf, 0]),
@@ -453,22 +454,26 @@
     outs = [weight_reduce(0, 30), weight_reduce(1, 32)]
 
     def own_out():
+        for cp in lm:
+            cp.wait()
         for m, out in enumerate((gu_out, gd_out)):
-            out[pl.ds(NF * hf, NF)] = g[z, j, hf, m]
+            out[pl.ds(NF * hf, NF)] = 0.9 * mom[m, pl.ds(NF * hf, NF)] + (1.0 / 64.0) * g[z, j, hf, m]
 
     def other_out():
         for m, out in enumerate((gu_out, gd_out)):
-            out[pl.ds(oh, NF)] = rc[m]
+            out[pl.ds(oh, NF)] = 0.9 * mom[m, pl.ds(oh, NF)] + (1.0 / 64.0) * rc[m]
 
     p.step("own_out", 0.1, own_out, outs[0][0] + outs[1][0])
     p.step("other_out", 0.1, other_out, outs[0][1] + outs[1][1])
     p.run()
 
 
-def finish(ig, gu, gd, mu, md, ig_out, mu_out, md_out):
-    ig_out[...] = ig[...]
-    mu_out[...] = 0.9 * mu[...] + (1.0 / 64.0) * gu[...]
-    md_out[...] = 0.9 * md[...] + (1.0 / 64.0) * gd[...]
+def finish(ig, mu, md, ig_out, mu_out, md_out, sem):
+    copies = [pltpu.make_async_copy(s, d, sem.at[n]) for n, (s, d) in enumerate(((ig, ig_out), (mu, mu_out), (md, md_out)))]
+    for cp in copies:
+        cp.start()
+    for cp in copies:
+        cp.wait()
 
 
 def shards(inputs, cotangent, up_blocks, down_blocks, up_index, down_index, mom_up, mom_down):
@@ -487,7 +492,7 @@
     ig, gu, gd = pl.pallas_call(
         kernel,
         out_shape=tuple(vm(*o.shape) for o in out_shape),
-        in_specs=[hbm] * 6,
+        in_specs=[hbm] * 8,
         out_specs=(vmem, vmem, vmem),
         scratch_shapes=[
             vm(2, 16, 32, 8, 128),
@@ -515,17 +520,18 @@
             pltpu.SMEM((NF, 32), jnp.int32),
             pltpu.SMEM((kb, f), jnp.int32),
             pltpu.SMEM((kb, f), jnp.int32),
-            pltpu.SemaphoreType.DMA((6,)),
+            vm(2, f, *tile),
+            pltpu.SemaphoreType.DMA((8,)),
             pltpu.SemaphoreType.DMA((NSEND,)),
             pltpu.SemaphoreType.DMA((NRECV,)),
         ],
         compiler_params=pltpu.CompilerParams(
             collective_id=0, has_side_effects=True, vmem_limit_bytes=60 * 1024 * 1024
         ),
-    )(up_index.T, down_index.T, rows8(inputs), rows8(cotangent), tiles(up_blocks), tiles(down_blocks))
-    ig, mu, md = pl.pallas_call(finish, out_shape=out_shape, in_specs=[vmem] * 5, out_specs=(vmem,) * 3)(
-        *(pltpu.with_memory_space_constraint(a, pltpu.VMEM) for a in (ig, gu, gd)), tiles(mom_up), tiles(mom_down)
-    )
+    )(up_index.T, down_index.T, rows8(inputs), rows8(cotangent), tiles(up_blocks), tiles(down_blocks), tiles(mom_up), tiles(mom_down))
+    ig, mu, md = pl.pallas_call(
+        finish, out_shape=out_shape, in_specs=[vmem] * 3, out_specs=(hbm,) * 3, scratch_shapes=[pltpu.SemaphoreType.DMA((3,))]
+    )(*(pltpu.with_memory_space_constraint(a, pltpu.VMEM) for a in (ig, gu, gd)))
     return ig, mu.reshape(mom_up.shape), md.reshape(mom_down.shape)
 
 

time: 81.7 us -> 80.7 us (0.988)
  Pallas kernels: 80.9 us -> 80 us
    pallas_call x1, Pallas kernels: 1.76 us -> 0.8 us  [shards(): pl.pallas_call(finish, out_shape=out_shape, in_specs=[vmem] * 3, out_spec...]
where the time goes in v6:
time: 80.7 us; the launch traced here: 80.6 us
  Pallas kernels  80 us (99%)
    pallas_call x1, Pallas kernels, shards(): pl.pallas_call(kernel, out_shape=tuple((vm(*o.shape) for o in out_shape))...  79.2 us

profile of v6, /device:TPU:32, one launch (start us, length us, event | category | flops | bytes accessed | tf_op | source)
XLA Modules:
  0.0 80.6 jit_solution(9176914160617015588)
XLA Ops:
  0.6 79.2 %shard_map.103 = (f32[128,512]{1,0:T(8,128)S(1)}, f32[14,2,8,128]{3,2,1,0:T(8,128)S(1)}, f32[14,2,8,128]{3,2,1,0:T(8,128)S(1)}) custom-call(s32[4,14]{1,0:T(4,128)} %bitcast.20, s32[4,14]{1,0:T(4,128)} %bitcast.21, f32[16,32,8,128]{3,2,1,0:T(8,128)} %bitcast.14, f32[16,32,8,128]{3,2,1,0:T(8,128)} %bitcast.15, f32[14,2,8,128]{3,2,1,0:T(8,128)} %bitcast.16, ...), custom_call_target="tpu_custom_call" | custom-call | tf_op jit(solution)/shard_map/pallas_call | solution.py:492
  79.8 0.8 shard_map.104
